TPU v7x, 32 devices: a whole 2x2x4 slice. The times are simulated.
32 devices in a mesh: groups: 2 (over y), ctx: 4 (over z), head: 4 (over x, core).
Axes of the slice: x: 2, y: 2, z: 4, core: 2. Of those that a mesh axis runs over, the one named last changes fastest.
Arguments:
- queries: bfloat16 [32768, 2048], P(('groups', 'ctx'), 'head'), parts along dimension 0, may hold values from -6 to 6
- key_vectors: bfloat16 [32768, 2048], P(('groups', 'ctx'), 'head'), parts along dimension 0, may hold values from -0.52734375 to 0.52734375
- value_vectors: bfloat16 [32768, 2048], P(('groups', 'ctx'), 'head'), parts along dimension 0, may hold values from -6 to 6
- token_rows: int32 [32768], P(('groups', 'ctx')), parts along dimension 0, may hold values from 0 to 63
- weight_table: float32 [64, 16, 21], P(None, 'head'), may hold values from 0.1 to 1
Outputs:
- attended: bfloat16 [32768, 2048], P(('groups', 'ctx'), 'head'), parts along dimension 0
There are 2 independent parts, one for each index of `groups`. A program takes and returns all parts, laid end to end along the dimension named above; an argument that names none is the same for every part. Nothing has to cross between parts.
All inputs are finite; a program needn't handle non-finite values.
Results may differ from a plain program's by a relative error of at most 0.004.
Values sent between devices are 32-bit elements; how exact they have to be, the bound alone decides.
No kernel may reach another device: no remote copies, remote signals or barrier semaphores. Data moves between devices by JAX's collectives and lax.ppermute only.
A program may use at most 128 MiB of HBM per device.

v0:
```python
import jax
import jax.numpy as jnp
from jax import lax
from jax.experimental import pallas as pl
from jax.experimental.pallas import tpu as pltpu
from jax.sharding import PartitionSpec as P

BLOCK = 256
HALF = BLOCK // 2
BLOCK_BITS = BLOCK.bit_length() - 1
ROWS = 8
ROW_BITS = ROWS.bit_length() - 1
TILES = HALF // ROWS
LANES = 128
SLOT = 32
PIECES = 4
FLIGHT = 2
MIB = 1 << 20
VMEM = pl.BlockSpec(memory_space=pltpu.VMEM)
HBM = pl.BlockSpec(memory_space=pltpu.HBM)
ROW_BY_ROW = (((1,), (1,)), ((), ()))


def columns(head):
    return pl.ds(head * LANES, LANES)


def level_weights(rows_ref, table_ref, weight_ref, local_bits):
    levels, heads, table_rows = table_ref.shape
    device = lax.axis_index("ctx")
    level = lax.broadcasted_iota(jnp.int32, (levels, table_rows), 0)
    scale = jnp.ones((levels, table_rows), jnp.float32)
    for level_id in range(2, levels):
        scale = jnp.where(level == level_id, 2.0 ** (-(level_id - 1) / 2), scale)
    for bit in range(lax.axis_size("ctx").bit_length() - 1):
        held = (device >> bit & 1).astype(jnp.float32)
        scale = jnp.where(level == local_bits + 1 + bit, scale * held, scale)
    slots = []
    for head in range(heads):
        slots.append(table_ref[:, head, :] * scale)
        slots.append(jnp.zeros((SLOT - levels, table_rows), jnp.float32))
    table = jnp.concatenate(slots, axis=0)
    high = table.astype(jnp.bfloat16)
    low = (table - high.astype(jnp.float32)).astype(jnp.bfloat16)
    ids = lax.broadcasted_iota(jnp.int32, (table_rows, BLOCK), 0)
    for start in range(0, weight_ref.shape[1], BLOCK):
        pick = (ids == rows_ref[:, start : start + BLOCK]).astype(jnp.float32).astype(jnp.bfloat16)
        weight_ref[:, start : start + BLOCK] = jnp.dot(
            high, pick, preferred_element_type=jnp.float32
        ) + jnp.dot(low, pick, preferred_element_type=jnp.float32)


def totals_kernel(heads, with_weights, follow, local_bits, *refs):
    refs = list(refs)
    key_hbm, value_hbm = refs.pop(0), refs.pop(0)
    small = [refs.pop(0), refs.pop(0)] if with_weights else []
    query_hbm = refs.pop(0) if follow is not None else None
    key_ref, turned_ref, left_ref, total_ref = (refs.pop(0) for _ in range(4))
    weight_ref = refs.pop(0) if with_weights else None
    query_ref = refs.pop(0) if follow is not None else None
    value_ref, sems = refs.pop(0), refs.pop(0)
    count = len(heads)
    token_count = key_ref.shape[1]
    block_count = token_count // BLOCK
    size = token_count // PIECES
    blocks = block_count // PIECES

    copies = []
    for place, head in enumerate(heads):
        for piece in range(PIECES):
            rows = pl.ds(piece * size, size)
            copies.append([
                pltpu.make_async_copy(
                    source.at[rows, columns(head)], target.at[place, rows, :], sems.at[len(copies), which]
                )
                for which, (source, target) in enumerate(((key_hbm, key_ref), (value_hbm, value_ref)))
            ])
    if with_weights:
        staged = [
            pltpu.make_async_copy(source, target, sems.at[len(copies), which])
            for which, (source, target) in enumerate(zip(small, refs))
        ]
        for copy in staged:
            copy.start()
    for step in range(FLIGHT):
        for copy in copies[step]:
            copy.start()
    if with_weights:
        for copy in staged:
            copy.wait()
        level_weights(refs[0], refs[1], weight_ref, local_bits)
    for step, pair in enumerate(copies):
        for copy in pair:
            copy.wait()
        if step + FLIGHT < len(copies):
            for copy in copies[step + FLIGHT]:
                copy.start()
        elif follow is not None and step + FLIGHT == len(copies):
            ahead = pltpu.make_async_copy(
                query_hbm.at[:, columns(follow)], query_ref, sems.at[len(copies), 0]
            )
            ahead.start()
        place, piece = divmod(step, PIECES)
        if piece == 0:
            held = {}
        for block in range(piece * blocks, (piece + 1) * blocks):
            rows = slice(block * BLOCK, (block + 1) * BLOCK)
            turned = jnp.transpose(value_ref[place, rows, :])
            turned_ref[place, :, rows] = turned
            carry = jnp.dot(turned, key_ref[place, rows, :], preferred_element_type=jnp.float32)
            bit = 0
            while block >> bit & 1:
                carry = carry + held.pop(bit)
                bit += 1
            held[bit] = carry
            if block + 1 < block_count:
                left_ref[place, block] = carry.astype(jnp.bfloat16)
            else:
                total_ref[place] = carry
    if follow is not None:
        ahead.wait()


def local_kernel(head, place, follow, *refs):
    query_ref, key_ref, turned_ref, left_ref, weight_ref = refs[:5]
    refs = list(refs[5:])
    query_hbm = refs.pop(0) if follow is not None else None
    part_ref = refs.pop(0)
    if follow is not None:
        next_ref = refs.pop(0)
        ahead = pltpu.make_async_copy(query_hbm.at[:, columns(follow)], next_ref, refs.pop(0))
        ahead.start()
    tile_ref = refs.pop(0)
    token_count = query_ref.shape[0]
    block_count = token_count // BLOCK
    base = head * SLOT

    lane = lax.broadcasted_iota(jnp.int32, (ROWS, HALF), 1)
    source = lax.broadcasted_iota(jnp.int32, (ROWS, HALF), 0)
    lane_tile = lane >> ROW_BITS
    near = (lane & ROWS - 1) ^ source
    behind = source > (lane & ROWS - 1)
    far_tile = lax.broadcasted_iota(jnp.int32, (TILES, HALF), 1) >> ROW_BITS
    far_source = lax.broadcasted_iota(jnp.int32, (TILES, HALF), 0)
    far = far_tile ^ far_source
    far_behind = far_source > far_tile

    def level_row(level, first, count):
        return weight_ref[base + level : base + level + 1, first : first + count]

    def own_half(scores, first, slot):
        chosen = jnp.broadcast_to(level_row(0, first, HALF), (ROWS, HALF))
        for bit in range(ROW_BITS):
            chosen = jnp.where(near >= 2**bit, level_row(1 + bit, first, HALF), chosen)
        chosen = jnp.where(behind, 0.0, chosen)
        spread = jnp.zeros((TILES, HALF), jnp.float32)
        for bit in range(BLOCK_BITS - 1 - ROW_BITS):
            spread = jnp.where(far >= 2**bit, level_row(1 + ROW_BITS + bit, first, HALF), spread)
        tile_ref[slot] = jnp.where(far_behind, 0.0, spread)
        rows = []
        for tile in range(TILES):
            weights = jnp.where(lane_tile == tile, chosen, tile_ref[slot, tile : tile + 1, :])
            rows.append(scores[tile * ROWS : (tile + 1) * ROWS] * weights)
        return jnp.concatenate(rows, axis=0).astype(jnp.bfloat16)

    for block in range(block_count):
        start = block * BLOCK
        rows = slice(start, start + BLOCK)
        bits = [bit for bit in range(block_count.bit_length() - 1) if block >> bit & 1]
        stacked = [key_ref[place, rows, :]] + [left_ref[place, (block >> bit << bit) - 1] for bit in bits]
        scores = lax.dot_general(
            jnp.concatenate(stacked, axis=0), query_ref[rows, :], ROW_BY_ROW,
            preferred_element_type=jnp.float32,
        )
        low = own_half(scores[:HALF, :HALF], start, 2 * block)
        high = own_half(scores[HALF:BLOCK, HALF:], start + HALF, 2 * block + 1)
        across = (scores[:HALF, HALF:] * level_row(BLOCK_BITS, start + HALF, HALF)).astype(jnp.bfloat16)
        weighted = jnp.concatenate(
            [
                jnp.concatenate([low, across], axis=1),
                jnp.concatenate([jnp.zeros_like(low), high], axis=1),
            ],
            axis=0,
        )
        result = jnp.dot(turned_ref[place, :, rows], weighted, preferred_element_type=jnp.float32)
        for spot, bit in enumerate(bits):
            first = BLOCK + spot * LANES
            result = result + scores[first : first + LANES] * level_row(BLOCK_BITS + 1 + bit, start, BLOCK)
        part_ref[:, rows] = result
    if follow is not None:
        ahead.wait()


def remote_kernel(heads, local_bits, bit_count, *refs):
    count = len(heads)
    weight_ref = refs[0]
    query_refs = refs[1 : 1 + count]
    part_refs = refs[1 + count : 1 + 2 * count]
    state_refs = refs[1 + 2 * count : 1 + 2 * count + bit_count]
    out_hbm, buffer, sems = refs[-3:]
    token_count = weight_ref.shape[1]
    size = token_count // PIECES
    copies = []
    for place, head in enumerate(heads):
        states = jnp.concatenate([ref[place] for ref in state_refs], axis=0).astype(jnp.bfloat16)
        for start in range(0, token_count, BLOCK):
            rows = slice(start, start + BLOCK)
            product = lax.dot_general(
                states, query_refs[place][rows, :], ROW_BY_ROW, preferred_element_type=jnp.float32
            )
            result = part_refs[place][:, rows]
            for bit in range(bit_count):
                row = head * SLOT + local_bits + 1 + bit
                result = result + product[bit * LANES : (bit + 1) * LANES] * weight_ref[row : row + 1, rows]
            buffer[place, rows, :] = jnp.transpose(result.astype(buffer.dtype))
            if (start + BLOCK) % size == 0:
                piece = pl.ds(start + BLOCK - size, size)
                copies.append(
                    pltpu.make_async_copy(
                        buffer.at[place, piece, :], out_hbm.at[piece, columns(head)], sems.at[len(copies)]
                    )
                )
                copies[-1].start()
    for copy in copies:
        copy.wait()


def join_kernel(left_ref, right_ref, out_ref):
    out_ref[...] = left_ref[...] + right_ref[...]


def sibling_totals(total, device_count):
    received = []
    for bit in range(device_count.bit_length() - 1):
        if bit:
            total = pl.pallas_call(
                join_kernel,
                in_specs=[VMEM, VMEM],
                out_specs=VMEM,
                out_shape=jax.ShapeDtypeStruct(total.shape, total.dtype),
                compiler_params=pltpu.CompilerParams(vmem_limit_bytes=2 * MIB),
                name="join",
            )(total, received[-1])
        pairs = [(device, device ^ 2**bit) for device in range(device_count)]
        received.append(lax.ppermute(total, "ctx", pairs))
    return received


def body(queries, key_vectors, value_vectors, token_rows, weight_table):
    table_rows, head_count, level_count = weight_table.shape
    token_count = queries.shape[0]
    width = queries.shape[1] // head_count
    block_count = token_count // BLOCK
    local_bits = token_count.bit_length() - 1
    bit_count = lax.axis_size("ctx").bit_length() - 1
    group = head_count // 2
    shape = jax.ShapeDtypeStruct
    whole = shape((token_count, width), jnp.bfloat16)
    params = pltpu.CompilerParams(vmem_limit_bytes=8 * MIB)
    in_hbm = lambda array: pltpu.with_memory_space_constraint(array, pltpu.HBM)
    queries, key_vectors, value_vectors = in_hbm(queries), in_hbm(key_vectors), in_hbm(value_vectors)
    small = (in_hbm(token_rows[None, :]), in_hbm(jnp.transpose(weight_table, (2, 1, 0))))

    keys, turned, lefts, received, query = [], [], [], [], {}
    for first in range(0, head_count, group):
        heads = tuple(range(first, first + group))
        with_weights = first == 0
        follow = 0 if first + group == head_count else None
        operands = [key_vectors, value_vectors]
        shapes = [
            shape((group, token_count, width), jnp.bfloat16),
            shape((group, width, token_count), jnp.bfloat16),
            shape((group, block_count, width, width), jnp.bfloat16),
            shape((group, width, width), jnp.float32),
        ]
        scratch = [
            pltpu.VMEM((group, token_count, width), jnp.bfloat16),
            pltpu.SemaphoreType.DMA((group * PIECES + 1, 2)),
        ]
        if with_weights:
            operands += small
            shapes.append(shape((head_count * SLOT, token_count), jnp.float32))
            scratch += [
                pltpu.VMEM((1, token_count), jnp.int32),
                pltpu.VMEM((level_count, head_count, table_rows), jnp.float32),
            ]
        if follow is not None:
            operands.append(queries)
            shapes.append(whole)
        results = pl.pallas_call(
            lambda *refs, args=(heads, with_weights, follow, local_bits): totals_kernel(*args, *refs),
            in_specs=[HBM] * len(operands),
            out_specs=[VMEM] * len(shapes),
            out_shape=shapes,
            scratch_shapes=scratch,
            compiler_params=params,
            name="totals",
        )(*operands)
        keys.append(results[0])
        turned.append(results[1])
        lefts.append(results[2])
        received.append(sibling_totals(results[3], lax.axis_size("ctx")))
        if with_weights:
            weights = results[4]
        if follow is not None:
            query[follow] = results[-1]

    parts = []
    for head in range(head_count):
        follow = head + 1 if head + 1 < head_count else None
        of = head // group
        results = pl.pallas_call(
            lambda *refs, args=(head, head % group, follow): local_kernel(*args, *refs),
            in_specs=[VMEM] * 5 + ([] if follow is None else [HBM]),
            out_specs=[VMEM] * (1 if follow is None else 2),
            out_shape=[shape((width, token_count), jnp.float32)] + ([] if follow is None else [whole]),
            scratch_shapes=([] if follow is None else [pltpu.SemaphoreType.DMA(())])
            + [pltpu.VMEM((2 * block_count, TILES, HALF), jnp.float32)],
            compiler_params=params,
            name="local",
        )(
            query[head], keys[of], turned[of], lefts[of], weights,
            *(() if follow is None else (queries,)),
        )
        parts.append(results[0])
        if follow is not None:
            query[follow] = results[1]

    out = None
    for first in range(0, head_count, group):
        heads = tuple(range(first, first + group))
        operands = [weights] + [query[head] for head in heads] + [parts[head] for head in heads]
        operands += received[first // group]
        out = pl.pallas_call(
            lambda *refs, heads=heads: remote_kernel(heads, local_bits, bit_count, *refs),
            in_specs=[VMEM] * len(operands) + ([] if out is None else [HBM]),
            out_specs=HBM,
            out_shape=shape(queries.shape, queries.dtype),
            input_output_aliases={} if out is None else {len(operands): 0},
            scratch_shapes=[
                pltpu.VMEM((group, token_count, width), jnp.bfloat16),
                pltpu.SemaphoreType.DMA((group * PIECES,)),
            ],
            compiler_params=params,
            name="remote",
        )(*operands, *(() if out is None else (out,)))
    return out


def solution(mesh):
    placed = (
        P(("groups", "ctx"), "head"),
        P(("groups", "ctx"), "head"),
        P(("groups", "ctx"), "head"),
        P(("groups", "ctx")),
        P(None, "head", None),
    )
    return jax.shard_map(
        body, mesh=mesh, in_specs=placed, out_specs=P(("groups", "ctx"), "head"), check_vma=False
    )
```

profile of v0, /device:TPU:0, one launch (start us, length us, event | category | flops | bytes accessed | tf_op | source)
XLA Modules:
  0.0 43.9 jit_solution(17901359394750172929)
XLA Ops:
  0.0 5.5 %totals.2 = (bf16[2,4096,128]{2,1,0:T(8,128)(2,1)S(1)}, bf16[2,128,4096]{2,1,0:T(8,128)(2,1)S(1)}, bf16[2,16,128,128]{3,2,1,0:T(8,128)(2,1)S(1)}, f32[2,128,128]{2,1,0:T(8,128)S(1)}, f32[128,4096]{1,0:T(8,128)S(1)}) custom-call(bf16[4096,512]{1,0:T(8,128)(2,1)} %refs_0_.3, bf16[4096,512]{1,0:T(8,128)(2,1)} %refs_1_.3, s32[1,4096]{1,0:T(1,128)} %bitcast.3, ...), custom_call_target="tpu_custom_call" | custom-call | tf_op jit(solution)/shard_map/totals/pallas_call | solution.py:290
  5.5 3.1 %collective-permute-start.2 = (f32[2,128,128]{2,1,0:T(8,128)S(1)}, f32[2,128,128]{2,1,0:T(8,128)S(1)}, u32[]{:S(2)}, u32[]{:S(2)}) collective-permute-start(f32[2,128,128]{2,1,0:T(8,128)S(1)} %get-tuple-element.36.left_ref), channel_id=1, source_target_pairs={{0,4},{4,0},{8,12},{12,8},{1,5},{5,1},{9,13},{13,9},{2,6},{6,2},{1... | collective-permute-start | bytes 393224 | tf_op jit(solution)/shard_map/ppermute | solution.py:245
  8.6 5.7 %totals.3 = (bf16[2,4096,128]{2,1,0:T(8,128)(2,1)S(1)}, bf16[2,128,4096]{2,1,0:T(8,128)(2,1)S(1)}, bf16[2,16,128,128]{3,2,1,0:T(8,128)(2,1)S(1)}, f32[2,128,128]{2,1,0:T(8,128)S(1)}, bf16[4096,128]{1,0:T(8,128)(2,1)S(1)}) custom-call(bf16[4096,512]{1,0:T(8,128)(2,1)} %refs_0_.3, bf16[4096,512]{1,0:T(8,128)(2,1)} %refs_1_.3, bf16[4096,512]{1,0:T(8,128)(2,1)} %refs_5_.5), custom_call_target="tpu_custom_call" | custom-call | tf_op jit(solution)/shard_map/totals/pallas_call | solution.py:290
  14.3 0.1 collective-permute-start
  14.4 0.0 collective-permute-done.2.right_ref.refs_5_
  14.4 3.1 %collective-permute-start.3 = (f32[2,128,128]{2,1,0:T(8,128)S(1)}, f32[2,128,128]{2,1,0:T(8,128)S(1)}, u32[]{:S(2)}, u32[]{:S(2)}) collective-permute-start(f32[2,128,128]{2,1,0:T(8,128)S(1)} %join.3), channel_id=1, source_target_pairs={{0,8},{4,12},{8,0},{12,4},{1,9},{5,13},{9,1},{13,5},{2,10},{6,14},... | collective-permute-start | bytes 393224 | tf_op jit(solution)/shard_map/ppermute | solution.py:245
  17.5 4.6 %collective-permute-done.right_ref.refs_5_ = f32[2,128,128]{2,1,0:T(8,128)S(1)} collective-permute-done((f32[2,128,128]{2,1,0:T(8,128)S(1)}, f32[2,128,128]{2,1,0:T(8,128)S(1)}, u32[]{:S(2)}, u32[]{:S(2)}) %collective-permute-start) | collective-permute-done | bytes 131104 | tf_op jit(solution)/shard_map/ppermute | solution.py:245
  22.1 1.2 %collective-permute-start.1 = (f32[2,128,128]{2,1,0:T(8,128)S(1)}, f32[2,128,128]{2,1,0:T(8,128)S(1)}, u32[]{:S(2)}, u32[]{:S(2)}) collective-permute-start(f32[2,128,128]{2,1,0:T(8,128)S(1)} %join.2), channel_id=1, source_target_pairs={{0,8},{4,12},{8,0},{12,4},{1,9},{5,13},{9,1},{13,5},{2,10},{6,14},... | collective-permute-start | bytes 393224 | tf_op jit(solution)/shard_map/ppermute | solution.py:245
  23.4 4.1 %local.4 = (f32[128,4096]{1,0:T(8,128)S(1)}, bf16[4096,128]{1,0:T(8,128)(2,1)S(1)}) custom-call(bf16[4096,128]{1,0:T(8,128)(2,1)S(1)} %get-tuple-element.22.refs_0_.refs_1_, bf16[2,4096,128]{2,1,0:T(8,128)(2,1)S(1)} %get-tuple-element.23.refs_1_, bf16[2,128,4096]{2,1,0:T(8,128)(2,1)S(1)} %get-tuple-element.24.refs_2_, ...), custom_call_target="tpu_custom_call" | custom-call | tf_op jit(solution)/shard_map/local/pallas_call | solution.py:312
  27.5 4.1 %local.5 = (f32[128,4096]{1,0:T(8,128)S(1)}, bf16[4096,128]{1,0:T(8,128)(2,1)S(1)}) custom-call(bf16[4096,128]{1,0:T(8,128)(2,1)S(1)} %get-tuple-element.26.refs_0_.refs_2_, bf16[2,4096,128]{2,1,0:T(8,128)(2,1)S(1)} %get-tuple-element.23.refs_1_, bf16[2,128,4096]{2,1,0:T(8,128)(2,1)S(1)} %get-tuple-element.24.refs_2_, ...), custom_call_target="tpu_custom_call" | custom-call | tf_op jit(solution)/shard_map/local/pallas_call | solution.py:312
  31.6 4.1 %local.6 = (f32[128,4096]{1,0:T(8,128)S(1)}, bf16[4096,128]{1,0:T(8,128)(2,1)S(1)}) custom-call(bf16[4096,128]{1,0:T(8,128)(2,1)S(1)} %get-tuple-element.27.refs_0_.refs_1_, bf16[2,4096,128]{2,1,0:T(8,128)(2,1)S(1)} %get-tuple-element.28.refs_1_, bf16[2,128,4096]{2,1,0:T(8,128)(2,1)S(1)} %get-tuple-element.29.refs_2_, ...), custom_call_target="tpu_custom_call" | custom-call | tf_op jit(solution)/shard_map/local/pallas_call | solution.py:312
  35.7 3.3 %local.7.refs_4_ = f32[128,4096]{1,0:T(8,128)S(1)} custom-call(bf16[4096,128]{1,0:T(8,128)(2,1)S(1)} %get-tuple-element.31.refs_0_.refs_2_, bf16[2,4096,128]{2,1,0:T(8,128)(2,1)S(1)} %get-tuple-element.28.refs_1_, bf16[2,128,4096]{2,1,0:T(8,128)(2,1)S(1)} %get-tuple-element.29.refs_2_, bf16[2,16,128,128]{3,2,1,0:T(8,128)(2,1)S(1)} %get-tuple-element.30.refs_3_, ...), custom_call_target="tpu_custom_call" | custom-call | tf_op jit(solution)/shard_map/local/pallas_call | solution.py:312
  39.1 0.0 collective-permute-done.3.refs_6_
  39.1 2.3 %remote.2.refs_7_ = bf16[4096,512]{1,0:T(8,128)(2,1)} custom-call(f32[128,4096]{1,0:T(8,128)S(1)} %get-tuple-element.21.refs_4_.refs_0_, bf16[4096,128]{1,0:T(8,128)(2,1)S(1)} %get-tuple-element.22.refs_0_.refs_1_, bf16[4096,128]{1,0:T(8,128)(2,1)S(1)} %get-tuple-element.26.refs_0_.refs_2_, f32[128,4096]{1,0:T(8,128)S(1)} %get-tuple-element.34.refs_3_, ...), custom_call_target="tpu_custom_call" | custom-call | tf_op jit(solution)/shard_map/remote/pallas_call | solution.py:334
  41.4 0.0 collective-permute-done.1.refs_6_
  41.4 2.3 %remote.3 = bf16[4096,512]{1,0:T(8,128)(2,1)} custom-call(f32[128,4096]{1,0:T(8,128)S(1)} %get-tuple-element.21.refs_4_.refs_0_, bf16[4096,128]{1,0:T(8,128)(2,1)S(1)} %get-tuple-element.27.refs_0_.refs_1_, bf16[4096,128]{1,0:T(8,128)(2,1)S(1)} %get-tuple-element.31.refs_0_.refs_2_, ...), custom_call_target="tpu_custom_call", output_to_operand_aliasing={{}: (7, {})} | custom-call | tf_op jit(solution)/shard_map/remote/pallas_call | solution.py:334
  (2 shorter events, 0.0 us)
Async XLA Ops:
  5.5 8.9 %collective-permute-start.2 = (f32[2,128,128]{2,1,0:T(8,128)S(1)}, f32[2,128,128]{2,1,0:T(8,128)S(1)}, u32[]{:S(2)}, u32[]{:S(2)}) collective-permute-start(f32[2,128,128]{2,1,0:T(8,128)S(1)} %get-tuple-element.36.left_ref), channel_id=1, source_target_pairs={{0,4},{4,0},{8,12},{12,8},{1,5},{5,1},{9,13},{13,9},{2,6},{6,2},{1... | collective-permute-start | bytes 393224 | tf_op jit(solution)/shard_map/ppermute | solution.py:245
  14.3 7.8 %collective-permute-start = (f32[2,128,128]{2,1,0:T(8,128)S(1)}, f32[2,128,128]{2,1,0:T(8,128)S(1)}, u32[]{:S(2)}, u32[]{:S(2)}) collective-permute-start(f32[2,128,128]{2,1,0:T(8,128)S(1)} %get-tuple-element.33.left_ref), channel_id=1, source_target_pairs={{0,4},{4,0},{8,12},{12,8},{1,5},{5,1},{9,13},{13,9},{2,6},{6,2},{1... | collective-permute-start | bytes 393224 | tf_op jit(solution)/shard_map/ppermute | solution.py:245
  14.4 24.7 %collective-permute-start.3 = (f32[2,128,128]{2,1,0:T(8,128)S(1)}, f32[2,128,128]{2,1,0:T(8,128)S(1)}, u32[]{:S(2)}, u32[]{:S(2)}) collective-permute-start(f32[2,128,128]{2,1,0:T(8,128)S(1)} %join.3), channel_id=1, source_target_pairs={{0,8},{4,12},{8,0},{12,4},{1,9},{5,13},{9,1},{13,5},{2,10},{6,14},... | collective-permute-start | bytes 393224 | tf_op jit(solution)/shard_map/ppermute | solution.py:245
  22.1 19.3 %collective-permute-start.1 = (f32[2,128,128]{2,1,0:T(8,128)S(1)}, f32[2,128,128]{2,1,0:T(8,128)S(1)}, u32[]{:S(2)}, u32[]{:S(2)}) collective-permute-start(f32[2,128,128]{2,1,0:T(8,128)S(1)} %join.2), channel_id=1, source_target_pairs={{0,8},{4,12},{8,0},{12,4},{1,9},{5,13},{9,1},{13,5},{2,10},{6,14},... | collective-permute-start | bytes 393224 | tf_op jit(solution)/shard_map/ppermute | solution.py:245
where the time goes:
time: 44.3 us; the launch traced here: 43.9 us
  Pallas kernels  31.4 us (71%)
  starting transfers between devices  7.53 us (17%)
  waiting for transfers between devices  4.65 us (10%)
    pallas_call x4, Pallas kernels, body(): pl.pallas_call(lambda *refs, args=(head, head % group, follow): local_ker...  15.6 us
    pallas_call x2, Pallas kernels, body(): pl.pallas_call(lambda *refs, args=(heads, with_weights, follow, local_bit...  11.2 us
    ppermute x4, starting transfers between devices, sibling_totals(): received.append(lax.ppermute(total, 'ctx', pairs))  7.53 us
    ppermute x4, waiting for transfers between devices, sibling_totals(): received.append(lax.ppermute(total, 'ctx', pairs))  4.65 us
    pallas_call x2, Pallas kernels, body(): pl.pallas_call(lambda *refs, heads=heads: remote_kernel(heads, local_bits...  4.61 us
  transfers between devices with their start and end apart: 4, of which 1 were waited for; matrix products, arithmetic and copies ran while one was open for 0% of the time, Pallas kernels for 54%

commit v1 on v0

v1 whole, which is shorter than its diff:
```python
import jax
import jax.numpy as jnp
from jax import lax
from jax.experimental import pallas as pl
from jax.experimental.pallas import tpu as pltpu
from jax.sharding import PartitionSpec as P

BLOCK = 256
HALF = BLOCK // 2
BLOCK_BITS = BLOCK.bit_length() - 1
ROWS = 8
ROW_BITS = ROWS.bit_length() - 1
TILES = HALF // ROWS
LANES = 128
SLOT = 32
PIECES = 8
GROUPS = 2
MIB = 1 << 20
VMEM = pl.BlockSpec(memory_space=pltpu.VMEM)
HBM = pl.BlockSpec(memory_space=pltpu.HBM)
ROW_BY_ROW = (((1,), (1,)), ((), ()))


def level_weights(rows_ref, table_ref, weight_ref, local_bits):
    levels, heads, table_rows = table_ref.shape
    device = lax.axis_index("ctx")
    level = lax.broadcasted_iota(jnp.int32, (levels, table_rows), 0)
    scale = jnp.ones((levels, table_rows), jnp.float32)
    for level_id in range(2, levels):
        scale = jnp.where(level == level_id, 2.0 ** (-(level_id - 1) / 2), scale)
    for bit in range(lax.axis_size("ctx").bit_length() - 1):
        held = (device >> bit & 1).astype(jnp.float32)
        scale = jnp.where(level == local_bits + 1 + bit, scale * held, scale)
    slots = []
    for head in range(heads):
        slots.append(table_ref[:, head, :] * scale)
        slots.append(jnp.zeros((SLOT - levels, table_rows), jnp.float32))
    table = jnp.concatenate(slots, axis=0)
    high = table.astype(jnp.bfloat16)
    low = (table - high.astype(jnp.float32)).astype(jnp.bfloat16)
    ids = lax.broadcasted_iota(jnp.int32, (table_rows, BLOCK), 0)
    for start in range(0, weight_ref.shape[1], BLOCK):
        pick = (ids == rows_ref[:, start : start + BLOCK]).astype(jnp.float32).astype(jnp.bfloat16)
        weight_ref[:, start : start + BLOCK] = jnp.dot(
            high, pick, preferred_element_type=jnp.float32
        ) + jnp.dot(low, pick, preferred_element_type=jnp.float32)


def pipelined(units, begin, finish):
    ahead = begin(units[0])
    for unit, following in zip(units, units[1:] + [None]):
        held, ahead = ahead, None if following is None else begin(following)
        finish(unit, held)


def totals_kernel(local_bits, key_hbm, value_hbm, rows_hbm, table_hbm, key_ref, turned_ref, left_ref, *refs):
    total_refs = refs[:GROUPS]
    weight_ref, value_ref, rows_ref, table_ref, sems, small_sems = refs[GROUPS:]
    token_count = key_ref.shape[0]
    head_count = turned_ref.shape[0]
    group = head_count // GROUPS
    block_count = token_count // BLOCK
    size = token_count // PIECES
    blocks = block_count // PIECES
    staged = [
        pltpu.make_async_copy(source, target, small_sems.at[which])
        for which, (source, target) in enumerate(((rows_hbm, rows_ref), (table_hbm, table_ref)))
    ]
    copies = []
    for piece in range(PIECES):
        rows = pl.ds(piece * size, size)
        copies.append([
            pltpu.make_async_copy(source.at[rows, :], target.at[rows, :], sems.at[piece, which])
            for which, (source, target) in enumerate(((key_hbm, key_ref), (value_hbm, value_ref)))
        ])
    for copy in staged + [copy for pair in copies for copy in pair]:
        copy.start()
    for copy in staged:
        copy.wait()
    level_weights(rows_ref, table_ref, weight_ref, local_bits)

    held = [{} for _ in range(head_count)]

    def begin(unit):
        block, head = unit
        rows = slice(block * BLOCK, (block + 1) * BLOCK)
        turned = jnp.transpose(value_ref[rows, head * LANES : (head + 1) * LANES])
        turned_ref[head, :, rows] = turned
        return turned

    def finish(unit, turned):
        block, head = unit
        rows = slice(block * BLOCK, (block + 1) * BLOCK)
        carry = jnp.dot(
            turned, key_ref[rows, head * LANES : (head + 1) * LANES], preferred_element_type=jnp.float32
        )
        bit = 0
        while block >> bit & 1:
            carry = carry + held[head].pop(bit)
            bit += 1
        held[head][bit] = carry
        if block + 1 < block_count:
            left_ref[head, block] = carry.astype(jnp.bfloat16)
        else:
            total_refs[head // group][head % group] = carry

    for piece, pair in enumerate(copies):
        for copy in pair:
            copy.wait()
        span = range(piece * blocks, (piece + 1) * blocks)
        pipelined([(block, head) for block in span for head in range(head_count)], begin, finish)


def local_kernel(head, loads, *refs):
    query_in, key_ref, turned_ref, left_ref, weight_ref, part_ref = refs[:6]
    refs = list(refs[6:])
    query_ref = refs.pop(0) if loads else query_in
    tile_ref = refs.pop(0)
    token_count = query_ref.shape[0]
    block_count = token_count // BLOCK
    columns = slice(head * LANES, (head + 1) * LANES)
    base = head * SLOT
    if loads:
        sems = refs.pop(0)
        size = token_count // PIECES
        copies = []
        for piece in range(PIECES):
            rows = pl.ds(piece * size, size)
            copies.append(pltpu.make_async_copy(query_in.at[rows, :], query_ref.at[rows, :], sems.at[piece]))
            copies[-1].start()

    lane = lax.broadcasted_iota(jnp.int32, (ROWS, HALF), 1)
    source = lax.broadcasted_iota(jnp.int32, (ROWS, HALF), 0)
    lane_tile = lane >> ROW_BITS
    near = (lane & ROWS - 1) ^ source
    behind = source > (lane & ROWS - 1)
    far_tile = lax.broadcasted_iota(jnp.int32, (TILES, HALF), 1) >> ROW_BITS
    far_source = lax.broadcasted_iota(jnp.int32, (TILES, HALF), 0)
    far = far_tile ^ far_source
    far_behind = far_source > far_tile

    def level_row(level, first, count):
        return weight_ref[base + level : base + level + 1, first : first + count]

    def own_half(scores, first, slot):
        chosen = jnp.broadcast_to(level_row(0, first, HALF), (ROWS, HALF))
        for bit in range(ROW_BITS):
            chosen = jnp.where(near >= 2**bit, level_row(1 + bit, first, HALF), chosen)
        chosen = jnp.where(behind, 0.0, chosen)
        spread = jnp.zeros((TILES, HALF), jnp.float32)
        for bit in range(BLOCK_BITS - 1 - ROW_BITS):
            spread = jnp.where(far >= 2**bit, level_row(1 + ROW_BITS + bit, first, HALF), spread)
        tile_ref[slot] = jnp.where(far_behind, 0.0, spread)
        rows = []
        for tile in range(TILES):
            weights = jnp.where(lane_tile == tile, chosen, tile_ref[slot, tile : tile + 1, :])
            rows.append(scores[tile * ROWS : (tile + 1) * ROWS] * weights)
        return jnp.concatenate(rows, axis=0).astype(jnp.bfloat16)

    def begin(block):
        rows = slice(block * BLOCK, (block + 1) * BLOCK)
        if loads and block % (block_count // PIECES) == 0:
            copies[block // (block_count // PIECES)].wait()
        query = jnp.transpose(query_ref[rows, columns])
        return query, jnp.dot(key_ref[rows, columns], query, preferred_element_type=jnp.float32)

    def finish(block, begun):
        query, scores = begun
        start = block * BLOCK
        rows = slice(start, start + BLOCK)
        low = own_half(scores[:HALF, :HALF], start, 2 * block)
        high = own_half(scores[HALF:, HALF:], start + HALF, 2 * block + 1)
        across = (scores[:HALF, HALF:] * level_row(BLOCK_BITS, start + HALF, HALF)).astype(jnp.bfloat16)
        right = [
            jnp.concatenate([low, across], axis=1),
            jnp.concatenate([jnp.zeros_like(low), high], axis=1),
        ]
        left = [turned_ref[head, :, rows]]
        for bit in range(block_count.bit_length() - 1):
            if block >> bit & 1:
                scaled = query.astype(jnp.float32) * level_row(BLOCK_BITS + 1 + bit, start, BLOCK)
                right.append(scaled.astype(jnp.bfloat16))
                left.append(left_ref[head, (block >> bit << bit) - 1])
        part_ref[:, rows] = jnp.dot(
            jnp.concatenate(left, axis=1), jnp.concatenate(right, axis=0),
            preferred_element_type=jnp.float32,
        )

    pipelined(list(range(block_count)), begin, finish)


def remote_kernel(heads, local_bits, bit_count, *refs):
    count = len(heads)
    weight_ref, query_ref = refs[:2]
    part_refs = refs[2 : 2 + count]
    state_refs = refs[2 + count : 2 + count + bit_count]
    out_hbm, buffer, sems = refs[-3:]
    token_count = weight_ref.shape[1]
    size = token_count // PIECES
    states = [
        jnp.concatenate([ref[place] for ref in state_refs], axis=0).astype(jnp.bfloat16)
        for place in range(count)
    ]
    copies = []

    def begin(unit):
        start, place = unit
        columns = slice(heads[place] * LANES, (heads[place] + 1) * LANES)
        return lax.dot_general(
            states[place], query_ref[start : start + BLOCK, columns], ROW_BY_ROW,
            preferred_element_type=jnp.float32,
        )

    def finish(unit, product):
        start, place = unit
        rows = slice(start, start + BLOCK)
        result = part_refs[place][:, rows]
        for bit in range(bit_count):
            row = heads[place] * SLOT + local_bits + 1 + bit
            result = result + product[bit * LANES : (bit + 1) * LANES] * weight_ref[row : row + 1, rows]
        buffer[rows, place * LANES : (place + 1) * LANES] = jnp.transpose(result.astype(buffer.dtype))
        if place + 1 == count and (start + BLOCK) % size == 0:
            piece = pl.ds(start + BLOCK - size, size)
            target = out_hbm.at[piece, pl.ds(heads[0] * LANES, count * LANES)]
            copies.append(pltpu.make_async_copy(buffer.at[piece, :], target, sems.at[len(copies)]))
            copies[-1].start()

    units = [(start, place) for start in range(0, token_count, BLOCK) for place in range(count)]
    pipelined(units, begin, finish)
    for copy in copies:
        copy.wait()


def join_kernel(left_ref, right_ref, after_ref, out_ref):
    out_ref[...] = left_ref[...] + right_ref[...]


def sibling_totals(total, device_count, after):
    received = []
    for bit in range(device_count.bit_length() - 1):
        if bit:
            total = pl.pallas_call(
                join_kernel,
                in_specs=[VMEM, VMEM, pl.BlockSpec(memory_space=pl.ANY)],
                out_specs=VMEM,
                out_shape=jax.ShapeDtypeStruct(total.shape, total.dtype),
                compiler_params=pltpu.CompilerParams(vmem_limit_bytes=2 * MIB),
                name="join",
            )(total, received[-1], after)
        pairs = [(device, device ^ 2**bit) for device in range(device_count)]
        received.append(lax.ppermute(total, "ctx", pairs))
    return received


def body(queries, key_vectors, value_vectors, token_rows, weight_table):
    table_rows, head_count, level_count = weight_table.shape
    token_count = queries.shape[0]
    width = queries.shape[1] // head_count
    block_count = token_count // BLOCK
    local_bits = token_count.bit_length() - 1
    devices = lax.axis_size("ctx")
    bit_count = devices.bit_length() - 1
    group = head_count // GROUPS
    shape = jax.ShapeDtypeStruct
    whole = shape(queries.shape, queries.dtype)
    params = pltpu.CompilerParams(vmem_limit_bytes=8 * MIB)
    in_hbm = lambda array: pltpu.with_memory_space_constraint(array, pltpu.HBM)
    queries, key_vectors, value_vectors = in_hbm(queries), in_hbm(key_vectors), in_hbm(value_vectors)

    keys, turned, lefts, *totals, weights = pl.pallas_call(
        lambda *refs: totals_kernel(local_bits, *refs),
        in_specs=[HBM] * 4,
        out_specs=[VMEM] * (4 + GROUPS),
        out_shape=[
            whole,
            shape((head_count, width, token_count), jnp.bfloat16),
            shape((head_count, block_count, width, width), jnp.bfloat16),
            *[shape((group, width, width), jnp.float32)] * GROUPS,
            shape((head_count * SLOT, token_count), jnp.float32),
        ],
        scratch_shapes=[
            pltpu.VMEM(queries.shape, queries.dtype),
            pltpu.VMEM((1, token_count), jnp.int32),
            pltpu.VMEM((level_count, head_count, table_rows), jnp.float32),
            pltpu.SemaphoreType.DMA((PIECES, 2)),
            pltpu.SemaphoreType.DMA((2,)),
        ],
        compiler_params=params,
        name="totals",
    )(key_vectors, value_vectors, in_hbm(token_rows[None, :]), in_hbm(jnp.transpose(weight_table, (2, 1, 0))))

    parts = []
    query = queries
    for head in range(head_count):
        loads = head == 0
        results = pl.pallas_call(
            lambda *refs, head=head, loads=loads: local_kernel(head, loads, *refs),
            in_specs=[HBM if loads else VMEM] + [VMEM] * 4,
            out_specs=[VMEM] * (2 if loads else 1),
            out_shape=[shape((width, token_count), jnp.float32)] + ([whole] if loads else []),
            scratch_shapes=[pltpu.VMEM((2 * block_count, TILES, HALF), jnp.float32)]
            + ([pltpu.SemaphoreType.DMA((PIECES,))] if loads else []),
            compiler_params=params,
            name="local",
        )(query, keys, turned, lefts, weights)
        parts.append(results[0])
        if loads:
            query = results[1]

    received = [sibling_totals(total, devices, parts[0]) for total in totals]
    out = None
    for first in range(0, head_count, group):
        heads = tuple(range(first, first + group))
        operands = [weights, query] + [parts[head] for head in heads] + received[first // group]
        out = pl.pallas_call(
            lambda *refs, heads=heads: remote_kernel(heads, local_bits, bit_count, *refs),
            in_specs=[VMEM] * len(operands) + ([] if out is None else [HBM]),
            out_specs=HBM,
            out_shape=whole,
            input_output_aliases={} if out is None else {len(operands): 0},
            scratch_shapes=[
                pltpu.VMEM((token_count, group * width), jnp.bfloat16),
                pltpu.SemaphoreType.DMA((PIECES,)),
            ],
            compiler_params=params,
            name="remote",
        )(*operands, *(() if out is None else (out,)))
    return out


def solution(mesh):
    placed = (
        P(("groups", "ctx"), "head"),
        P(("groups", "ctx"), "head"),
        P(("groups", "ctx"), "head"),
        P(("groups", "ctx")),
        P(None, "head", None),
    )
    return jax.shard_map(
        body, mesh=mesh, in_specs=placed, out_specs=P(("groups", "ctx"), "head"), check_vma=False
    )
```

time: 44.3 us -> 32.3 us (0.73)
  Pallas kernels: 31.4 us -> 21 us
  waiting for transfers between devices: 4.65 us -> 3.59 us
    pallas_call x8 -> x7, Pallas kernels: 26.8 us -> 16.4 us  [the longest x4 9.55 us: body(): pl.pallas_call(lambda *refs, head=head, loads=loads: local_kernel(head, l...]
    ppermute x4, waiting for transfers between devices: 4.65 us -> 3.59 us  [sibling_totals(): received.append(lax.ppermute(total, 'ctx', pairs))]
  transfers between devices with their start and end apart: 4 -> 4, of which waited for: 1 -> 1; matrix products, arithmetic and copies ran while one was open for 0% -> 0% of each run, Pallas kernels for 54% -> 37%
where the time goes in v1:
time: 32.3 us; the launch traced here: 32.2 us
  Pallas kernels  21 us (65%)
  starting transfers between devices  7.49 us (23%)
  waiting for transfers between devices  3.59 us (11%)
    pallas_call x4, Pallas kernels, body(): pl.pallas_call(lambda *refs, head=head, loads=loads: local_kernel(head, l...  9.55 us
    ppermute x4, starting transfers between devices, sibling_totals(): received.append(lax.ppermute(total, 'ctx', pairs))  7.49 us
    pallas_call x1, Pallas kernels, body(): pl.pallas_call(lambda *refs: totals_kernel(local_bits, *refs), in_specs=[...  6.85 us
    pallas_call x2, Pallas kernels, body(): pl.pallas_call(lambda *refs, heads=heads: remote_kernel(heads, local_bits...  4.6 us
    ppermute x4, waiting for transfers between devices, sibling_totals(): received.append(lax.ppermute(total, 'ctx', pairs))  3.59 us
  transfers between devices with their start and end apart: 4, of which 1 were waited for; matrix products, arithmetic and copies ran while one was open for 0% of the time, Pallas kernels for 37%

profile of v1, /device:TPU:0, one launch (start us, length us, event | category | flops | bytes accessed | tf_op | source)
XLA Modules:
  0.0 32.2 jit_solution(6823970747150511977)
XLA Ops:
  0.0 6.9 %totals.1 = (bf16[4096,512]{1,0:T(8,128)(2,1)S(1)}, bf16[4,128,4096]{2,1,0:T(8,128)(2,1)S(1)}, bf16[4,16,128,128]{3,2,1,0:T(8,128)(2,1)S(1)}, f32[2,128,128]{2,1...) custom-call(bf16[4096,512]{1,0:T(8,128)(2,1)} %refs_0_.2, bf16[4096,512]{1,0:T(8,128)(2,1)} %refs_1_.1, ...), custom_call_target="tpu_custom_call" | custom-call | tf_op jit(solution)/shard_map/totals/pallas_call | solution.py:270
  6.9 3.1 %collective-permute-start.2 = (f32[2,128,128]{2,1,0:T(8,128)S(1)}, f32[2,128,128]{2,1,0:T(8,128)S(1)}, u32[]{:S(2)}, u32[]{:S(2)}) collective-permute-start(f32[2,128,128]{2,1,0:T(8,128)S(1)} %get-tuple-element.20.left_ref), channel_id=1, source_target_pairs={{0,4},{4,0},{8,12},{12,8},{1,5},{5,1},{9,13},{13,9},{2,6},{6,2},{1... | collective-permute-start | bytes 393224 | tf_op jit(solution)/shard_map/ppermute | solution.py:251
  10.0 0.1 collective-permute-start
  10.1 4.7 %local.4 = (f32[128,4096]{1,0:T(8,128)S(1)}, bf16[4096,512]{1,0:T(8,128)(2,1)S(1)}) custom-call(bf16[4096,512]{1,0:T(8,128)(2,1)} %refs_0_.3, bf16[4096,512]{1,0:T(8,128)(2,1)S(1)} %get-tuple-element.14.refs_1_, bf16[4,128,4096]{2,1,0:T(8,128)(2,1)S(1)} %get-tuple-element.15.refs_2_, bf16[4,16,128,128]{3,2,1,0:T(8,128)(2,1)S(1)} %get-tuple-element.16.refs_3_, ...), custom_call_target="tpu_custom_call" | custom-call | tf_op jit(solution)/shard_map/local/pallas_call | solution.py:296
  14.8 0.0 collective-permute-done.2.right_ref.refs_4_
  14.8 3.0 %collective-permute-start.3 = (f32[2,128,128]{2,1,0:T(8,128)S(1)}, f32[2,128,128]{2,1,0:T(8,128)S(1)}, u32[]{:S(2)}, u32[]{:S(2)}) collective-permute-start(f32[2,128,128]{2,1,0:T(8,128)S(1)} %join.3), channel_id=1, source_target_pairs={{0,8},{4,12},{8,0},{12,4},{1,9},{5,13},{9,1},{13,5},{2,10},{6,14},... | collective-permute-start | bytes 393224 | tf_op jit(solution)/shard_map/ppermute | solution.py:251
  17.8 0.0 collective-permute-done.right_ref.refs_4_
  17.9 1.3 %collective-permute-start.1 = (f32[2,128,128]{2,1,0:T(8,128)S(1)}, f32[2,128,128]{2,1,0:T(8,128)S(1)}, u32[]{:S(2)}, u32[]{:S(2)}) collective-permute-start(f32[2,128,128]{2,1,0:T(8,128)S(1)} %join.2), channel_id=1, source_target_pairs={{0,8},{4,12},{8,0},{12,4},{1,9},{5,13},{9,1},{13,5},{2,10},{6,14},... | collective-permute-start | bytes 393224 | tf_op jit(solution)/shard_map/ppermute | solution.py:251
  19.1 1.6 %local.7.refs_3_ = f32[128,4096]{1,0:T(8,128)S(1)} custom-call(bf16[4096,512]{1,0:T(8,128)(2,1)S(1)} %get-tuple-element.17.refs_0_.refs_1_, bf16[4096,512]{1,0:T(8,128)(2,1)S(1)} %get-tuple-element.14.refs_1_, bf16[4,128,4096]{2,1,0:T(8,128)(2,1)S(1)} %get-tuple-element.15.refs_2_, bf16[4,16,128,128]{3,2,1,0:T(8,128)(2,1)S(1)} %get-tuple-element.16.refs_3_, ...), custom_call_target="tpu_custom_call" | custom-call | tf_op jit(solution)/shard_map/local/pallas_call | solution.py:296
  20.7 1.6 %local.6.refs_3_ = f32[128,4096]{1,0:T(8,128)S(1)} custom-call(bf16[4096,512]{1,0:T(8,128)(2,1)S(1)} %get-tuple-element.17.refs_0_.refs_1_, bf16[4096,512]{1,0:T(8,128)(2,1)S(1)} %get-tuple-element.14.refs_1_, bf16[4,128,4096]{2,1,0:T(8,128)(2,1)S(1)} %get-tuple-element.15.refs_2_, bf16[4,16,128,128]{3,2,1,0:T(8,128)(2,1)S(1)} %get-tuple-element.16.refs_3_, ...), custom_call_target="tpu_custom_call" | custom-call | tf_op jit(solution)/shard_map/local/pallas_call | solution.py:296
  22.4 1.6 %local.5.refs_2_ = f32[128,4096]{1,0:T(8,128)S(1)} custom-call(bf16[4096,512]{1,0:T(8,128)(2,1)S(1)} %get-tuple-element.17.refs_0_.refs_1_, bf16[4096,512]{1,0:T(8,128)(2,1)S(1)} %get-tuple-element.14.refs_1_, bf16[4,128,4096]{2,1,0:T(8,128)(2,1)S(1)} %get-tuple-element.15.refs_2_, bf16[4,16,128,128]{3,2,1,0:T(8,128)(2,1)S(1)} %get-tuple-element.16.refs_3_, ...), custom_call_target="tpu_custom_call" | custom-call | tf_op jit(solution)/shard_map/local/pallas_call | solution.py:296
  24.0 3.6 %collective-permute-done.3.refs_5_ = f32[2,128,128]{2,1,0:T(8,128)S(1)} collective-permute-done((f32[2,128,128]{2,1,0:T(8,128)S(1)}, f32[2,128,128]{2,1,0:T(8,128)S(1)}, u32[]{:S(2)}, u32[]{:S(2)}) %collective-permute-start.3) | collective-permute-done | bytes 131104 | tf_op jit(solution)/shard_map/ppermute | solution.py:251
  27.6 2.3 %remote.2.refs_6_ = bf16[4096,512]{1,0:T(8,128)(2,1)} custom-call(f32[128,4096]{1,0:T(8,128)S(1)} %get-tuple-element.13.refs_4_.refs_0_, bf16[4096,512]{1,0:T(8,128)(2,1)S(1)} %get-tuple-element.17.refs_0_.refs_1_, f32[128,4096]{1,0:T(8,128)S(1)} %get-tuple-element.19.after_ref.refs_2_, f32[128,4096]{1,0:T(8,128)S(1)} %local.7.refs_3_, ...), custom_call_target="tpu_custom_call" | custom-call | tf_op jit(solution)/shard_map/remote/pallas_call | solution.py:315
  29.9 0.0 collective-permute-done.1.refs_5_
  29.9 2.3 %remote.3 = bf16[4096,512]{1,0:T(8,128)(2,1)} custom-call(f32[128,4096]{1,0:T(8,128)S(1)} %get-tuple-element.13.refs_4_.refs_0_, bf16[4096,512]{1,0:T(8,128)(2,1)S(1)} %get-tuple-element.17.refs_0_.refs_1_, f32[128,4096]{1,0:T(8,128)S(1)} %local.5.refs_2_, f32[128,4096]{1,0:T(8,128)S(1)} %local.6.refs_3_, ...), custom_call_target="tpu_custom_call", output_to_operand_aliasing={{}: (6, {})} | custom-call | tf_op jit(solution)/shard_map/remote/pallas_call | solution.py:315
  (2 shorter events, 0.0 us)
Async XLA Ops:
  6.9 7.9 %collective-permute-start.2 = (f32[2,128,128]{2,1,0:T(8,128)S(1)}, f32[2,128,128]{2,1,0:T(8,128)S(1)}, u32[]{:S(2)}, u32[]{:S(2)}) collective-permute-start(f32[2,128,128]{2,1,0:T(8,128)S(1)} %get-tuple-element.20.left_ref), channel_id=1, source_target_pairs={{0,4},{4,0},{8,12},{12,8},{1,5},{5,1},{9,13},{13,9},{2,6},{6,2},{1... | collective-permute-start | bytes 393224 | tf_op jit(solution)/shard_map/ppermute | solution.py:251
  10.0 7.9 %collective-permute-start = (f32[2,128,128]{2,1,0:T(8,128)S(1)}, f32[2,128,128]{2,1,0:T(8,128)S(1)}, u32[]{:S(2)}, u32[]{:S(2)}) collective-permute-start(f32[2,128,128]{2,1,0:T(8,128)S(1)} %get-tuple-element.18.left_ref), channel_id=1, source_target_pairs={{0,4},{4,0},{8,12},{12,8},{1,5},{5,1},{9,13},{13,9},{2,6},{6,2},{1... | collective-permute-start | bytes 393224 | tf_op jit(solution)/shard_map/ppermute | solution.py:251
  14.8 12.7 %collective-permute-start.3 = (f32[2,128,128]{2,1,0:T(8,128)S(1)}, f32[2,128,128]{2,1,0:T(8,128)S(1)}, u32[]{:S(2)}, u32[]{:S(2)}) collective-permute-start(f32[2,128,128]{2,1,0:T(8,128)S(1)} %join.3), channel_id=1, source_target_pairs={{0,8},{4,12},{8,0},{12,4},{1,9},{5,13},{9,1},{13,5},{2,10},{6,14},... | collective-permute-start | bytes 393224 | tf_op jit(solution)/shard_map/ppermute | solution.py:251
  17.9 12.0 %collective-permute-start.1 = (f32[2,128,128]{2,1,0:T(8,128)S(1)}, f32[2,128,128]{2,1,0:T(8,128)S(1)}, u32[]{:S(2)}, u32[]{:S(2)}) collective-permute-start(f32[2,128,128]{2,1,0:T(8,128)S(1)} %join.2), channel_id=1, source_target_pairs={{0,8},{4,12},{8,0},{12,4},{1,9},{5,13},{9,1},{13,5},{2,10},{6,14},... | collective-permute-start | bytes 393224 | tf_op jit(solution)/shard_map/ppermute | solution.py:251

commit v2 on v1

--- a/solution.py
+++ b/solution.py
@@ -18,6 +18,7 @@
 MIB = 1 << 20
 VMEM = pl.BlockSpec(memory_space=pltpu.VMEM)
 HBM = pl.BlockSpec(memory_space=pltpu.HBM)
+ANY = pl.BlockSpec(memory_space=pl.ANY)
 ROW_BY_ROW = (((1,), (1,)), ((), ()))
 
 
@@ -53,19 +54,15 @@
         finish(unit, held)
 
 
-def totals_kernel(local_bits, key_hbm, value_hbm, rows_hbm, table_hbm, key_ref, turned_ref, left_ref, *refs):
+def totals_kernel(key_hbm, value_hbm, key_ref, turned_ref, left_ref, *refs):
     total_refs = refs[:GROUPS]
-    weight_ref, value_ref, rows_ref, table_ref, sems, small_sems = refs[GROUPS:]
+    value_ref, sems = refs[GROUPS:]
     token_count = key_ref.shape[0]
     head_count = turned_ref.shape[0]
     group = head_count // GROUPS
     block_count = token_count // BLOCK
     size = token_count // PIECES
     blocks = block_count // PIECES
-    staged = [
-        pltpu.make_async_copy(source, target, small_sems.at[which])
-        for which, (source, target) in enumerate(((rows_hbm, rows_ref), (table_hbm, table_ref)))
-    ]
     copies = []
     for piece in range(PIECES):
         rows = pl.ds(piece * size, size)
@@ -73,11 +70,9 @@
             pltpu.make_async_copy(source.at[rows, :], target.at[rows, :], sems.at[piece, which])
             for which, (source, target) in enumerate(((key_hbm, key_ref), (value_hbm, value_ref)))
         ])
-    for copy in staged + [copy for pair in copies for copy in pair]:
-        copy.start()
-    for copy in staged:
-        copy.wait()
-    level_weights(rows_ref, table_ref, weight_ref, local_bits)
+    for pair in copies:
+        for copy in pair:
+            copy.start()
 
     held = [{} for _ in range(head_count)]
 
@@ -111,23 +106,30 @@
         pipelined([(block, head) for block in span for head in range(head_count)], begin, finish)
 
 
-def local_kernel(head, loads, *refs):
-    query_in, key_ref, turned_ref, left_ref, weight_ref, part_ref = refs[:6]
-    refs = list(refs[6:])
-    query_ref = refs.pop(0) if loads else query_in
-    tile_ref = refs.pop(0)
+def prepare_kernel(local_bits, after_ref, query_hbm, rows_hbm, table_hbm, weight_ref, query_ref, *refs):
+    rows_ref, table_ref, sems = refs
+    small = [
+        pltpu.make_async_copy(rows_hbm, rows_ref, sems.at[0]),
+        pltpu.make_async_copy(table_hbm, table_ref, sems.at[1]),
+    ]
+    large = pltpu.make_async_copy(query_hbm, query_ref, sems.at[2])
+    for copy in small + [large]:
+        copy.start()
+    for copy in small:
+        copy.wait()
+    level_weights(rows_ref, table_ref, weight_ref, local_bits)
+    large.wait()
+
+
+def local_kernel(head, place, local_bits, *refs):
+    query_ref, key_ref, turned_ref, left_ref, weight_ref = refs[:5]
+    state_refs = refs[5:-2]
+    part_ref, tile_ref = refs[-2:]
     token_count = query_ref.shape[0]
     block_count = token_count // BLOCK
     columns = slice(head * LANES, (head + 1) * LANES)
     base = head * SLOT
-    if loads:
-        sems = refs.pop(0)
-        size = token_count // PIECES
-        copies = []
-        for piece in range(PIECES):
-            rows = pl.ds(piece * size, size)
-            copies.append(pltpu.make_async_copy(query_in.at[rows, :], query_ref.at[rows, :], sems.at[piece]))
-            copies[-1].start()
+    states = [(local_bits + 1 + bit, ref[place].astype(jnp.bfloat16)) for bit, ref in enumerate(state_refs)]
 
     lane = lax.broadcasted_iota(jnp.int32, (ROWS, HALF), 1)
     source = lax.broadcasted_iota(jnp.int32, (ROWS, HALF), 0)
@@ -159,8 +161,6 @@
 
     def begin(block):
         rows = slice(block * BLOCK, (block + 1) * BLOCK)
-        if loads and block % (block_count // PIECES) == 0:
-            copies[block // (block_count // PIECES)].wait()
         query = jnp.transpose(query_ref[rows, columns])
         return query, jnp.dot(key_ref[rows, columns], query, preferred_element_type=jnp.float32)
 
@@ -176,11 +176,15 @@
             jnp.concatenate([jnp.zeros_like(low), high], axis=1),
         ]
         left = [turned_ref[head, :, rows]]
-        for bit in range(block_count.bit_length() - 1):
-            if block >> bit & 1:
-                scaled = query.astype(jnp.float32) * level_row(BLOCK_BITS + 1 + bit, start, BLOCK)
-                right.append(scaled.astype(jnp.bfloat16))
-                left.append(left_ref[head, (block >> bit << bit) - 1])
+        terms = [
+            (BLOCK_BITS + 1 + bit, left_ref[head, (block >> bit << bit) - 1])
+            for bit in range(block_count.bit_length() - 1)
+            if block >> bit & 1
+        ]
+        for level, sibling in terms + states:
+            scaled = query.astype(jnp.float32) * level_row(level, start, BLOCK)
+            right.append(scaled.astype(jnp.bfloat16))
+            left.append(sibling)
         part_ref[:, rows] = jnp.dot(
             jnp.concatenate(left, axis=1), jnp.concatenate(right, axis=0),
             preferred_element_type=jnp.float32,
@@ -189,18 +193,15 @@
     pipelined(list(range(block_count)), begin, finish)
 
 
-def remote_kernel(heads, local_bits, bit_count, *refs):
+def remote_kernel(heads, level, *refs):
     count = len(heads)
     weight_ref, query_ref = refs[:2]
     part_refs = refs[2 : 2 + count]
-    state_refs = refs[2 + count : 2 + count + bit_count]
+    state_ref = refs[2 + count]
     out_hbm, buffer, sems = refs[-3:]
     token_count = weight_ref.shape[1]
     size = token_count // PIECES
-    states = [
-        jnp.concatenate([ref[place] for ref in state_refs], axis=0).astype(jnp.bfloat16)
-        for place in range(count)
-    ]
+    states = [state_ref[place].astype(jnp.bfloat16) for place in range(count)]
     copies = []
 
     def begin(unit):
@@ -214,10 +215,8 @@
     def finish(unit, product):
         start, place = unit
         rows = slice(start, start + BLOCK)
-        result = part_refs[place][:, rows]
-        for bit in range(bit_count):
-            row = heads[place] * SLOT + local_bits + 1 + bit
-            result = result + product[bit * LANES : (bit + 1) * LANES] * weight_ref[row : row + 1, rows]
+        row = heads[place] * SLOT + level
+        result = part_refs[place][:, rows] + product * weight_ref[row : row + 1, rows]
         buffer[rows, place * LANES : (place + 1) * LANES] = jnp.transpose(result.astype(buffer.dtype))
         if place + 1 == count and (start + BLOCK) % size == 0:
             piece = pl.ds(start + BLOCK - size, size)
@@ -235,21 +234,20 @@
     out_ref[...] = left_ref[...] + right_ref[...]
 
 
-def sibling_totals(total, device_count, after):
-    received = []
-    for bit in range(device_count.bit_length() - 1):
-        if bit:
-            total = pl.pallas_call(
-                join_kernel,
-                in_specs=[VMEM, VMEM, pl.BlockSpec(memory_space=pl.ANY)],
-                out_specs=VMEM,
-                out_shape=jax.ShapeDtypeStruct(total.shape, total.dtype),
-                compiler_params=pltpu.CompilerParams(vmem_limit_bytes=2 * MIB),
-                name="join",
-            )(total, received[-1], after)
-        pairs = [(device, device ^ 2**bit) for device in range(device_count)]
-        received.append(lax.ppermute(total, "ctx", pairs))
-    return received
+def join(total, received, after):
+    return pl.pallas_call(
+        join_kernel,
+        in_specs=[VMEM, VMEM, ANY],
+        out_specs=VMEM,
+        out_shape=jax.ShapeDtypeStruct(total.shape, total.dtype),
+        compiler_params=pltpu.CompilerParams(vmem_limit_bytes=2 * MIB),
+        name="join",
+    )(total, received, after)
+
+
+def exchange(total, bit):
+    devices = lax.axis_size("ctx")
+    return lax.ppermute(total, "ctx", [(device, device ^ 2**bit) for device in range(devices)])
 
 
 def body(queries, key_vectors, value_vectors, token_rows, weight_table):
@@ -267,53 +265,63 @@
     in_hbm = lambda array: pltpu.with_memory_space_constraint(array, pltpu.HBM)
     queries, key_vectors, value_vectors = in_hbm(queries), in_hbm(key_vectors), in_hbm(value_vectors)
 
-    keys, turned, lefts, *totals, weights = pl.pallas_call(
-        lambda *refs: totals_kernel(local_bits, *refs),
-        in_specs=[HBM] * 4,
-        out_specs=[VMEM] * (4 + GROUPS),
+    keys, turned, lefts, *totals = pl.pallas_call(
+        totals_kernel,
+        in_specs=[HBM] * 2,
+        out_specs=[VMEM] * (3 + GROUPS),
         out_shape=[
             whole,
             shape((head_count, width, token_count), jnp.bfloat16),
             shape((head_count, block_count, width, width), jnp.bfloat16),
             *[shape((group, width, width), jnp.float32)] * GROUPS,
-            shape((head_count * SLOT, token_count), jnp.float32),
         ],
         scratch_shapes=[
             pltpu.VMEM(queries.shape, queries.dtype),
-            pltpu.VMEM((1, token_count), jnp.int32),
-            pltpu.VMEM((level_count, head_count, table_rows), jnp.float32),
             pltpu.SemaphoreType.DMA((PIECES, 2)),
-            pltpu.SemaphoreType.DMA((2,)),
         ],
         compiler_params=params,
         name="totals",
-    )(key_vectors, value_vectors, in_hbm(token_rows[None, :]), in_hbm(jnp.transpose(weight_table, (2, 1, 0))))
-
+    )(key_vectors, value_vectors)
+
+    weights, query = pl.pallas_call(
+        lambda *refs: prepare_kernel(local_bits, *refs),
+        in_specs=[ANY] + [HBM] * 3,
+        out_specs=[VMEM] * 2,
+        out_shape=[shape((head_count * SLOT, token_count), jnp.float32), whole],
+        scratch_shapes=[
+            pltpu.VMEM((1, token_count), jnp.int32),
+            pltpu.VMEM((level_count, head_count, table_rows), jnp.float32),
+            pltpu.SemaphoreType.DMA((3,)),
+        ],
+        compiler_params=params,
+        name="prepare",
+    )(lefts, queries, in_hbm(token_rows[None, :]), in_hbm(jnp.transpose(weight_table, (2, 1, 0))))
+
+    received = [[exchange(total, 0)] for total in totals]
     parts = []
-    query = queries
-    for head in range(head_count):
-        loads = head == 0
-        results = pl.pallas_call(
-            lambda *refs, head=head, loads=loads: local_kernel(head, loads, *refs),
-            in_specs=[HBM if loads else VMEM] + [VMEM] * 4,
-            out_specs=[VMEM] * (2 if loads else 1),
-            out_shape=[shape((width, token_count), jnp.float32)] + ([whole] if loads else []),
-            scratch_shapes=[pltpu.VMEM((2 * block_count, TILES, HALF), jnp.float32)]
-            + ([pltpu.SemaphoreType.DMA((PIECES,))] if loads else []),
-            compiler_params=params,
-            name="local",
-        )(query, keys, turned, lefts, weights)
-        parts.append(results[0])
-        if loads:
-            query = results[1]
-
-    received = [sibling_totals(total, devices, parts[0]) for total in totals]
+    after = weights
+    for index, total in enumerate(totals):
+        for bit in range(1, bit_count):
+            total = join(total, received[index][-1], after)
+            received[index].append(exchange(total, bit))
+        for head in range(index * group, (index + 1) * group):
+            parts += pl.pallas_call(
+                lambda *refs, head=head: local_kernel(head, head % group, local_bits, *refs),
+                in_specs=[VMEM] * (5 + bit_count - 1),
+                out_specs=[VMEM],
+                out_shape=[shape((width, token_count), jnp.float32)],
+                scratch_shapes=[pltpu.VMEM((2 * block_count, TILES, HALF), jnp.float32)],
+                compiler_params=params,
+                name="local",
+            )(query, keys, turned, lefts, weights, *received[index][:-1])
+        after = parts[0]
+
     out = None
-    for first in range(0, head_count, group):
-        heads = tuple(range(first, first + group))
-        operands = [weights, query] + [parts[head] for head in heads] + received[first // group]
+    for index, arrived in enumerate(received):
+        heads = tuple(range(index * group, (index + 1) * group))
+        operands = [weights, query] + [parts[head] for head in heads] + [arrived[-1]]
         out = pl.pallas_call(
-            lambda *refs, heads=heads: remote_kernel(heads, local_bits, bit_count, *refs),
+            lambda *refs, heads=heads: remote_kernel(heads, local_bits + bit_count, *refs),
             in_specs=[VMEM] * len(operands) + ([] if out is None else [HBM]),
             out_specs=HBM,
             out_shape=whole,

time: 32.3 us -> 27.3 us (0.85)
  Pallas kernels: 21 us -> 17.4 us
  waiting for transfers between devices: 3.59 us -> 2.35 us
    pallas_call x7 -> x8, Pallas kernels: 16.4 us -> 14 us  [the longest x4 7.56 us: body(): pl.pallas_call(lambda *refs, head=head: local_kernel(head, head % group,...]
    ppermute x4, waiting for transfers between devices: 3.59 us -> 2.35 us  [exchange(): lax.ppermute(total, 'ctx', [(device, device ^ 2 ** bit) for device in ran...]
    pallas_call x2, Pallas kernels: 4.6 us -> 3.37 us  [body(): pl.pallas_call(lambda *refs, heads=heads: remote_kernel(heads, local_bits...]
  transfers between devices with their start and end apart: 4 -> 4, of which waited for: 1 -> 2; matrix products, arithmetic and copies ran while one was open for 0% -> 0% of each run, Pallas kernels for 37% -> 43%
where the time goes in v2:
time: 27.3 us; the launch traced here: 27 us
  Pallas kernels  17.4 us (64%)
  starting transfers between devices  7.18 us (26%)
  waiting for transfers between devices  2.35 us (9%)
    pallas_call x4, Pallas kernels, body(): pl.pallas_call(lambda *refs, head=head: local_kernel(head, head % group,...  7.56 us
    ppermute x4, starting transfers between devices, exchange(): lax.ppermute(total, 'ctx', [(device, device ^ 2 ** bit) for device in ran...  7.18 us
    pallas_call x1, Pallas kernels, body(): pl.pallas_call(totals_kernel, in_specs=[HBM] * 2, out_specs=[VMEM] * (3 +...  4.19 us
    pallas_call x2, Pallas kernels, body(): pl.pallas_call(lambda *refs, heads=heads: remote_kernel(heads, local_bits...  3.37 us
    ppermute x4, waiting for transfers between devices, exchange(): lax.ppermute(total, 'ctx', [(device, device ^ 2 ** bit) for device in ran...  2.35 us
    pallas_call x1, Pallas kernels, body(): pl.pallas_call(lambda *refs: prepare_kernel(local_bits, *refs), in_specs=...  2.26 us
  transfers between devices with their start and end apart: 4, of which 2 were waited for; matrix products, arithmetic and copies ran while one was open for 0% of the time, Pallas kernels for 43%

profile of v2, /device:TPU:0, one launch (start us, length us, event | category | flops | bytes accessed | tf_op | source)
XLA Modules:
  0.0 27.0 jit_solution(2453253616689747662)
XLA Ops:
  0.0 4.2 %totals.1 = (bf16[4096,512]{1,0:T(8,128)(2,1)S(1)}, bf16[4,128,4096]{2,1,0:T(8,128)(2,1)S(1)}, bf16[4,16,128,128]{3,2,1,0:T(8,128)(2,1)S(1)}, f32[2,128,128]{2,1,0:T(8,128)S(1)}, f32[2,128,128]{2,1,0:T(8,128)S(1)}) custom-call(bf16[4096,512]{1,0:T(8,128)(2,1)} %key_hbm.1, bf16[4096,512]{1,0:T(8,128)(2,1)} %value_hbm.1), custom_call_target="tpu_custom_call" | custom-call | tf_op jit(solution)/shard_map/totals/pallas_call | solution.py:268
  4.2 3.1 %collective-permute-start.1 = (f32[2,128,128]{2,1,0:T(8,128)S(1)}, f32[2,128,128]{2,1,0:T(8,128)S(1)}, u32[]{:S(2)}, u32[]{:S(2)}) collective-permute-start(f32[2,128,128]{2,1,0:T(8,128)S(1)} %get-tuple-element.18.left_ref), channel_id=1, source_target_pairs={{0,4},{4,0},{8,12},{12,8},{1,5},{5,1},{9,13},{13,9},{2,6},{6,2},{1... | collective-permute-start | bytes 393224 | tf_op jit(solution)/shard_map/ppermute | solution.py:250
  7.3 0.1 collective-permute-start
  7.4 2.3 %prepare.1 = (f32[128,4096]{1,0:T(8,128)S(1)}, bf16[4096,512]{1,0:T(8,128)(2,1)S(1)}) custom-call(bf16[4,16,128,128]{3,2,1,0:T(8,128)(2,1)S(1)} %get-tuple-element.12.refs_0_.refs_3_, bf16[4096,512]{1,0:T(8,128)(2,1)} %refs_1_.1, s32[1,4096]{1,0:T(1,128)} %bitcast.3, f32[21,4,64]{2,1,0:T(4,128)} %bitcast.2), custom_call_target="tpu_custom_call" | custom-call | tf_op jit(solution)/shard_map/prepare/pallas_call | solution.py:286
  9.7 2.0 %collective-permute-done.1.refs_5_.right_ref = f32[2,128,128]{2,1,0:T(8,128)S(1)} collective-permute-done((f32[2,128,128]{2,1,0:T(8,128)S(1)}, f32[2,128,128]{2,1,0:T(8,128)S(1)}, u32[]{:S(2)}, u32[]{:S(2)}) %collective-permute-start.1) | collective-permute-done | bytes 131104 | tf_op jit(solution)/shard_map/ppermute | solution.py:250
  11.7 3.1 %collective-permute-start.3 = (f32[2,128,128]{2,1,0:T(8,128)S(1)}, f32[2,128,128]{2,1,0:T(8,128)S(1)}, u32[]{:S(2)}, u32[]{:S(2)}) collective-permute-start(f32[2,128,128]{2,1,0:T(8,128)S(1)} %join.3), channel_id=1, source_target_pairs={{0,8},{4,12},{8,0},{12,4},{1,9},{5,13},{9,1},{13,5},{2,10},{6,14},... | collective-permute-start | bytes 393224 | tf_op jit(solution)/shard_map/ppermute | solution.py:250
  14.8 1.9 %local.6.after_ref.refs_2_ = f32[128,4096]{1,0:T(8,128)S(1)} custom-call(bf16[4096,512]{1,0:T(8,128)(2,1)S(1)} %get-tuple-element.14.refs_0_.refs_1_, bf16[4096,512]{1,0:T(8,128)(2,1)S(1)} %get-tuple-element.15.refs_1_, bf16[4,128,4096]{2,1,0:T(8,128)(2,1)S(1)} %get-tuple-element.16.refs_2_, bf16[4,16,128,128]{3,2,1,0:T(8,128)(2,1)S(1)} %get-tuple-element.12.refs_0_.refs_3_, ...), custom_call_target="tpu_custom_call" | custom-call | tf_op jit(solution)/shard_map/local/pallas_call | solution.py:308
  16.7 0.0 collective-permute-done.refs_5_.right_ref
  16.7 0.9 %collective-permute-start.2 = (f32[2,128,128]{2,1,0:T(8,128)S(1)}, f32[2,128,128]{2,1,0:T(8,128)S(1)}, u32[]{:S(2)}, u32[]{:S(2)}) collective-permute-start(f32[2,128,128]{2,1,0:T(8,128)S(1)} %join.2), channel_id=1, source_target_pairs={{0,8},{4,12},{8,0},{12,4},{1,9},{5,13},{9,1},{13,5},{2,10},{6,14},... | collective-permute-start | bytes 393224 | tf_op jit(solution)/shard_map/ppermute | solution.py:250
  17.6 1.9 %local.7.refs_3_ = f32[128,4096]{1,0:T(8,128)S(1)} custom-call(bf16[4096,512]{1,0:T(8,128)(2,1)S(1)} %get-tuple-element.14.refs_0_.refs_1_, bf16[4096,512]{1,0:T(8,128)(2,1)S(1)} %get-tuple-element.15.refs_1_, bf16[4,128,4096]{2,1,0:T(8,128)(2,1)S(1)} %get-tuple-element.16.refs_2_, bf16[4,16,128,128]{3,2,1,0:T(8,128)(2,1)S(1)} %get-tuple-element.12.refs_0_.refs_3_, ...), custom_call_target="tpu_custom_call" | custom-call | tf_op jit(solution)/shard_map/local/pallas_call | solution.py:308
  19.5 1.9 %local.5.refs_3_ = f32[128,4096]{1,0:T(8,128)S(1)} custom-call(bf16[4096,512]{1,0:T(8,128)(2,1)S(1)} %get-tuple-element.14.refs_0_.refs_1_, bf16[4096,512]{1,0:T(8,128)(2,1)S(1)} %get-tuple-element.15.refs_1_, bf16[4,128,4096]{2,1,0:T(8,128)(2,1)S(1)} %get-tuple-element.16.refs_2_, bf16[4,16,128,128]{3,2,1,0:T(8,128)(2,1)S(1)} %get-tuple-element.12.refs_0_.refs_3_, ...), custom_call_target="tpu_custom_call" | custom-call | tf_op jit(solution)/shard_map/local/pallas_call | solution.py:308
  21.4 1.9 %local.4.refs_2_ = f32[128,4096]{1,0:T(8,128)S(1)} custom-call(bf16[4096,512]{1,0:T(8,128)(2,1)S(1)} %get-tuple-element.14.refs_0_.refs_1_, bf16[4096,512]{1,0:T(8,128)(2,1)S(1)} %get-tuple-element.15.refs_1_, bf16[4,128,4096]{2,1,0:T(8,128)(2,1)S(1)} %get-tuple-element.16.refs_2_, bf16[4,16,128,128]{3,2,1,0:T(8,128)(2,1)S(1)} %get-tuple-element.12.refs_0_.refs_3_, ...), custom_call_target="tpu_custom_call" | custom-call | tf_op jit(solution)/shard_map/local/pallas_call | solution.py:308
  23.3 0.0 collective-permute-done.3.refs_4_
  23.3 1.7 %remote.2.refs_5_ = bf16[4096,512]{1,0:T(8,128)(2,1)} custom-call(f32[128,4096]{1,0:T(8,128)S(1)} %get-tuple-element.13.refs_4_.after_ref.refs_0_, bf16[4096,512]{1,0:T(8,128)(2,1)S(1)} %get-tuple-element.14.refs_0_.refs_1_, f32[128,4096]{1,0:T(8,128)S(1)} %local.6.after_ref.refs_2_, f32[128,4096]{1,0:T(8,128)S(1)} %local.7.refs_3_, ...), custom_call_target="tpu_custom_call" | custom-call | tf_op jit(solution)/shard_map/remote/pallas_call | solution.py:323
  25.0 0.3 %collective-permute-done.2.refs_4_ = f32[2,128,128]{2,1,0:T(8,128)S(1)} collective-permute-done((f32[2,128,128]{2,1,0:T(8,128)S(1)}, f32[2,128,128]{2,1,0:T(8,128)S(1)}, u32[]{:S(2)}, u32[]{:S(2)}) %collective-permute-start.2) | collective-permute-done | bytes 131104 | tf_op jit(solution)/shard_map/ppermute | solution.py:250
  25.3 1.7 %remote.3 = bf16[4096,512]{1,0:T(8,128)(2,1)} custom-call(f32[128,4096]{1,0:T(8,128)S(1)} %get-tuple-element.13.refs_4_.after_ref.refs_0_, bf16[4096,512]{1,0:T(8,128)(2,1)S(1)} %get-tuple-element.14.refs_0_.refs_1_, f32[128,4096]{1,0:T(8,128)S(1)} %local.4.refs_2_, f32[128,4096]{1,0:T(8,128)S(1)} %local.5.refs_3_, ...), custom_call_target="tpu_custom_call", output_to_operand_aliasing={{}: (5, {})} | custom-call | tf_op jit(solution)/shard_map/remote/pallas_call | solution.py:323
  (2 shorter events, 0.0 us)
Async XLA Ops:
  4.2 7.5 %collective-permute-start.1 = (f32[2,128,128]{2,1,0:T(8,128)S(1)}, f32[2,128,128]{2,1,0:T(8,128)S(1)}, u32[]{:S(2)}, u32[]{:S(2)}) collective-permute-start(f32[2,128,128]{2,1,0:T(8,128)S(1)} %get-tuple-element.18.left_ref), channel_id=1, source_target_pairs={{0,4},{4,0},{8,12},{12,8},{1,5},{5,1},{9,13},{13,9},{2,6},{6,2},{1... | collective-permute-start | bytes 393224 | tf_op jit(solution)/shard_map/ppermute | solution.py:250
  7.3 9.4 %collective-permute-start = (f32[2,128,128]{2,1,0:T(8,128)S(1)}, f32[2,128,128]{2,1,0:T(8,128)S(1)}, u32[]{:S(2)}, u32[]{:S(2)}) collective-permute-start(f32[2,128,128]{2,1,0:T(8,128)S(1)} %get-tuple-element.17.left_ref), channel_id=1, source_target_pairs={{0,4},{4,0},{8,12},{12,8},{1,5},{5,1},{9,13},{13,9},{2,6},{6,2},{1... | collective-permute-start | bytes 393224 | tf_op jit(solution)/shard_map/ppermute | solution.py:250
  11.7 11.6 %collective-permute-start.3 = (f32[2,128,128]{2,1,0:T(8,128)S(1)}, f32[2,128,128]{2,1,0:T(8,128)S(1)}, u32[]{:S(2)}, u32[]{:S(2)}) collective-permute-start(f32[2,128,128]{2,1,0:T(8,128)S(1)} %join.3), channel_id=1, source_target_pairs={{0,8},{4,12},{8,0},{12,4},{1,9},{5,13},{9,1},{13,5},{2,10},{6,14},... | collective-permute-start | bytes 393224 | tf_op jit(solution)/shard_map/ppermute | solution.py:250
  16.7 8.6 %collective-permute-start.2 = (f32[2,128,128]{2,1,0:T(8,128)S(1)}, f32[2,128,128]{2,1,0:T(8,128)S(1)}, u32[]{:S(2)}, u32[]{:S(2)}) collective-permute-start(f32[2,128,128]{2,1,0:T(8,128)S(1)} %join.2), channel_id=1, source_target_pairs={{0,8},{4,12},{8,0},{12,4},{1,9},{5,13},{9,1},{13,5},{2,10},{6,14},... | collective-permute-start | bytes 393224 | tf_op jit(solution)/shard_map/ppermute | solution.py:250

commit v3 on v2

--- a/solution.py
+++ b/solution.py
@@ -22,7 +22,7 @@
 ROW_BY_ROW = (((1,), (1,)), ((), ()))
 
 
-def level_weights(rows_ref, table_ref, weight_ref, local_bits):
+def scaled_table(table_ref, local_bits):
     levels, heads, table_rows = table_ref.shape
     device = lax.axis_index("ctx")
     level = lax.broadcasted_iota(jnp.int32, (levels, table_rows), 0)
@@ -38,13 +38,7 @@
         slots.append(jnp.zeros((SLOT - levels, table_rows), jnp.float32))
     table = jnp.concatenate(slots, axis=0)
     high = table.astype(jnp.bfloat16)
-    low = (table - high.astype(jnp.float32)).astype(jnp.bfloat16)
-    ids = lax.broadcasted_iota(jnp.int32, (table_rows, BLOCK), 0)
-    for start in range(0, weight_ref.shape[1], BLOCK):
-        pick = (ids == rows_ref[:, start : start + BLOCK]).astype(jnp.float32).astype(jnp.bfloat16)
-        weight_ref[:, start : start + BLOCK] = jnp.dot(
-            high, pick, preferred_element_type=jnp.float32
-        ) + jnp.dot(low, pick, preferred_element_type=jnp.float32)
+    return high, (table - high.astype(jnp.float32)).astype(jnp.bfloat16)
 
 
 def pipelined(units, begin, finish):
@@ -54,9 +48,9 @@
         finish(unit, held)
 
 
-def totals_kernel(key_hbm, value_hbm, key_ref, turned_ref, left_ref, *refs):
+def totals_kernel(local_bits, key_hbm, value_hbm, rows_hbm, table_hbm, key_ref, turned_ref, left_ref, weight_ref, *refs):
     total_refs = refs[:GROUPS]
-    value_ref, sems = refs[GROUPS:]
+    value_ref, rows_ref, table_ref, sems, small_sems = refs[GROUPS:]
     token_count = key_ref.shape[0]
     head_count = turned_ref.shape[0]
     group = head_count // GROUPS
@@ -70,9 +64,12 @@
             pltpu.make_async_copy(source.at[rows, :], target.at[rows, :], sems.at[piece, which])
             for which, (source, target) in enumerate(((key_hbm, key_ref), (value_hbm, value_ref)))
         ])
-    for pair in copies:
-        for copy in pair:
-            copy.start()
+    staged = [
+        pltpu.make_async_copy(source, target, small_sems.at[which])
+        for which, (source, target) in enumerate(((rows_hbm, rows_ref), (table_hbm, table_ref)))
+    ]
+    for copy in copies[0] + staged + [copy for pair in copies[1:] for copy in pair]:
+        copy.start()
 
     held = [{} for _ in range(head_count)]
 
@@ -102,23 +99,21 @@
     for piece, pair in enumerate(copies):
         for copy in pair:
             copy.wait()
+        if piece == 1:
+            for copy in staged:
+                copy.wait()
+            high, low = scaled_table(table_ref, local_bits)
+        if piece >= 1:
+            first = 0 if piece == 1 else piece * blocks
+            ids = lax.broadcasted_iota(jnp.int32, (high.shape[1], BLOCK), 0)
+            for block in range(first, (piece + 1) * blocks):
+                tokens = slice(block * BLOCK, (block + 1) * BLOCK)
+                pick = (ids == rows_ref[:, tokens]).astype(jnp.float32).astype(jnp.bfloat16)
+                weight_ref[:, tokens] = jnp.dot(
+                    high, pick, preferred_element_type=jnp.float32
+                ) + jnp.dot(low, pick, preferred_element_type=jnp.float32)
         span = range(piece * blocks, (piece + 1) * blocks)
         pipelined([(block, head) for block in span for head in range(head_count)], begin, finish)
-
-
-def prepare_kernel(local_bits, after_ref, query_hbm, rows_hbm, table_hbm, weight_ref, query_ref, *refs):
-    rows_ref, table_ref, sems = refs
-    small = [
-        pltpu.make_async_copy(rows_hbm, rows_ref, sems.at[0]),
-        pltpu.make_async_copy(table_hbm, table_ref, sems.at[1]),
-    ]
-    large = pltpu.make_async_copy(query_hbm, query_ref, sems.at[2])
-    for copy in small + [large]:
-        copy.start()
-    for copy in small:
-        copy.wait()
-    level_weights(rows_ref, table_ref, weight_ref, local_bits)
-    large.wait()
 
 
 def local_kernel(head, place, local_bits, *refs):
@@ -193,15 +188,18 @@
     pipelined(list(range(block_count)), begin, finish)
 
 
-def remote_kernel(heads, level, *refs):
+def remote_kernel(heads, levels, *refs):
     count = len(heads)
     weight_ref, query_ref = refs[:2]
     part_refs = refs[2 : 2 + count]
-    state_ref = refs[2 + count]
+    state_refs = refs[2 + count : 2 + count + len(levels)]
     out_hbm, buffer, sems = refs[-3:]
     token_count = weight_ref.shape[1]
     size = token_count // PIECES
-    states = [state_ref[place].astype(jnp.bfloat16) for place in range(count)]
+    states = [
+        jnp.concatenate([ref[place] for ref in state_refs], axis=0).astype(jnp.bfloat16)
+        for place in range(count)
+    ]
     copies = []
 
     def begin(unit):
@@ -215,8 +213,10 @@
     def finish(unit, product):
         start, place = unit
         rows = slice(start, start + BLOCK)
-        row = heads[place] * SLOT + level
-        result = part_refs[place][:, rows] + product * weight_ref[row : row + 1, rows]
+        result = part_refs[place][:, rows]
+        for spot, level in enumerate(levels):
+            row = heads[place] * SLOT + level
+            result = result + product[spot * LANES : (spot + 1) * LANES] * weight_ref[row : row + 1, rows]
         buffer[rows, place * LANES : (place + 1) * LANES] = jnp.transpose(result.astype(buffer.dtype))
         if place + 1 == count and (start + BLOCK) % size == 0:
             piece = pl.ds(start + BLOCK - size, size)
@@ -230,19 +230,19 @@
         copy.wait()
 
 
-def join_kernel(left_ref, right_ref, after_ref, out_ref):
-    out_ref[...] = left_ref[...] + right_ref[...]
+def join_kernel(left_ref, right_ref, *refs):
+    refs[-1][...] = left_ref[...] + right_ref[...]
 
 
 def join(total, received, after):
     return pl.pallas_call(
         join_kernel,
-        in_specs=[VMEM, VMEM, ANY],
+        in_specs=[VMEM, VMEM] + [ANY] * len(after),
         out_specs=VMEM,
         out_shape=jax.ShapeDtypeStruct(total.shape, total.dtype),
         compiler_params=pltpu.CompilerParams(vmem_limit_bytes=2 * MIB),
         name="join",
-    )(total, received, after)
+    )(total, received, *after)
 
 
 def exchange(total, bit):
@@ -263,65 +263,61 @@
     whole = shape(queries.shape, queries.dtype)
     params = pltpu.CompilerParams(vmem_limit_bytes=8 * MIB)
     in_hbm = lambda array: pltpu.with_memory_space_constraint(array, pltpu.HBM)
-    queries, key_vectors, value_vectors = in_hbm(queries), in_hbm(key_vectors), in_hbm(value_vectors)
-
-    keys, turned, lefts, *totals = pl.pallas_call(
-        totals_kernel,
-        in_specs=[HBM] * 2,
-        out_specs=[VMEM] * (3 + GROUPS),
+    key_vectors, value_vectors = in_hbm(key_vectors), in_hbm(value_vectors)
+
+    keys, turned, lefts, weights, *totals = pl.pallas_call(
+        lambda *refs: totals_kernel(local_bits, *refs),
+        in_specs=[HBM] * 4,
+        out_specs=[VMEM] * (4 + GROUPS),
         out_shape=[
             whole,
             shape((head_count, width, token_count), jnp.bfloat16),
             shape((head_count, block_count, width, width), jnp.bfloat16),
+            shape((head_count * SLOT, token_count), jnp.float32),
             *[shape((group, width, width), jnp.float32)] * GROUPS,
         ],
         scratch_shapes=[
             pltpu.VMEM(queries.shape, queries.dtype),
+            pltpu.VMEM((1, token_count), jnp.int32),
+            pltpu.VMEM((level_count, head_count, table_rows), jnp.float32),
             pltpu.SemaphoreType.DMA((PIECES, 2)),
+            pltpu.SemaphoreType.DMA((2,)),
         ],
         compiler_params=params,
         name="totals",
-    )(key_vectors, value_vectors)
-
-    weights, query = pl.pallas_call(
-        lambda *refs: prepare_kernel(local_bits, *refs),
-        in_specs=[ANY] + [HBM] * 3,
-        out_specs=[VMEM] * 2,
-        out_shape=[shape((head_count * SLOT, token_count), jnp.float32), whole],
-        scratch_shapes=[
-            pltpu.VMEM((1, token_count), jnp.int32),
-            pltpu.VMEM((level_count, head_count, table_rows), jnp.float32),
-            pltpu.SemaphoreType.DMA((3,)),
-        ],
-        compiler_params=params,
-        name="prepare",
-    )(lefts, queries, in_hbm(token_rows[None, :]), in_hbm(jnp.transpose(weight_table, (2, 1, 0))))
+    )(key_vectors, value_vectors, in_hbm(token_rows[None, :]), in_hbm(jnp.transpose(weight_table, (2, 1, 0))))
+
+    def local(head, states):
+        return pl.pallas_call(
+            lambda *refs: local_kernel(head, head % group, local_bits, *refs),
+            in_specs=[VMEM] * (5 + len(states)),
+            out_specs=VMEM,
+            out_shape=shape((width, token_count), jnp.float32),
+            scratch_shapes=[pltpu.VMEM((2 * block_count, TILES, HALF), jnp.float32)],
+            compiler_params=params,
+            name="local",
+        )(queries, keys, turned, lefts, weights, *states)
 
     received = [[exchange(total, 0)] for total in totals]
-    parts = []
-    after = weights
+    parts, after = [], []
     for index, total in enumerate(totals):
+        members = range(index * group, (index + 1) * group)
+        if index == 0:
+            parts += [local(head, []) for head in members]
         for bit in range(1, bit_count):
-            total = join(total, received[index][-1], after)
+            total = join(total, received[index][-1], parts[index : index + 1])
             received[index].append(exchange(total, bit))
-        for head in range(index * group, (index + 1) * group):
-            parts += pl.pallas_call(
-                lambda *refs, head=head: local_kernel(head, head % group, local_bits, *refs),
-                in_specs=[VMEM] * (5 + bit_count - 1),
-                out_specs=[VMEM],
-                out_shape=[shape((width, token_count), jnp.float32)],
-                scratch_shapes=[pltpu.VMEM((2 * block_count, TILES, HALF), jnp.float32)],
-                compiler_params=params,
-                name="local",
-            )(query, keys, turned, lefts, weights, *received[index][:-1])
-        after = parts[0]
+        if index:
+            parts += [local(head, received[index][:-1]) for head in members]
 
     out = None
     for index, arrived in enumerate(received):
         heads = tuple(range(index * group, (index + 1) * group))
-        operands = [weights, query] + [parts[head] for head in heads] + [arrived[-1]]
+        first = bit_count - 1 if index else 0
+        levels = tuple(range(local_bits + 1 + first, local_bits + 1 + bit_count))
+        operands = [weights, queries] + [parts[head] for head in heads] + arrived[first:]
         out = pl.pallas_call(
-            lambda *refs, heads=heads: remote_kernel(heads, local_bits + bit_count, *refs),
+            lambda *refs, heads=heads, levels=levels: remote_kernel(heads, levels, *refs),
             in_specs=[VMEM] * len(operands) + ([] if out is None else [HBM]),
             out_specs=HBM,
             out_shape=whole,

time: 27.3 us -> 30.1 us (1.10)
  starting transfers between devices: 7.18 us -> 8.88 us
  waiting for transfers between devices: 2.35 us -> 3.82 us
    ppermute x4, starting transfers between devices: 7.18 us -> 8.88 us  [exchange(): lax.ppermute(total, 'ctx', [(device, device ^ 2 ** bit) for device in ran...]
    ppermute x4, waiting for transfers between devices: 2.35 us -> 3.82 us  [exchange(): lax.ppermute(total, 'ctx', [(device, device ^ 2 ** bit) for device in ran...]
    pallas_call x10 -> x9, Pallas kernels: 17.4 us -> 17.1 us  [the longest x4 7 us: local(): pl.pallas_call(lambda *refs: local_kernel(head, head % group, local_bits,...]
  transfers between devices with their start and end apart: 4 -> 4, of which waited for: 2 -> 2; matrix products, arithmetic and copies ran while one was open for 0% -> 0% of each run, Pallas kernels for 43% -> 31%
where the time goes in v3:
time: 30.1 us; the launch traced here: 29.9 us
  Pallas kernels  17.1 us (57%)
  starting transfers between devices  8.88 us (30%)
  waiting for transfers between devices  3.82 us (13%)
    ppermute x4, starting transfers between devices, exchange(): lax.ppermute(total, 'ctx', [(device, device ^ 2 ** bit) for device in ran...  8.88 us
    pallas_call x4, Pallas kernels, local(): pl.pallas_call(lambda *refs: local_kernel(head, head % group, local_bits,...  7 us
    pallas_call x1, Pallas kernels, body(): pl.pallas_call(lambda *refs: totals_kernel(local_bits, *refs), in_specs=[...  6.13 us
    pallas_call x2, Pallas kernels, body(): pl.pallas_call(lambda *refs, heads=heads, levels=levels: remote_kernel(he...  3.99 us
    ppermute x4, waiting for transfers between devices, exchange(): lax.ppermute(total, 'ctx', [(device, device ^ 2 ** bit) for device in ran...  3.82 us
  transfers between devices with their start and end apart: 4, of which 2 were waited for; matrix products, arithmetic and copies ran while one was open for 0% of the time, Pallas kernels for 31%

profile of v3, /device:TPU:0, one launch (start us, length us, event | category | flops | bytes accessed | tf_op | source)
XLA Modules:
  0.0 29.9 jit_solution(11930539074472331989)
XLA Ops:
  0.0 0.0 copy-start
  0.0 6.1 %totals.1 = (bf16[4096,512]{1,0:T(8,128)(2,1)S(1)}, bf16[4,128,4096]{2,1,0:T(8,128)(2,1)S(1)}, bf16[4,16,128,128]{3,2,1,0:T(8,128)(2,1)S(1)}, f32[128,4096]{1,0:...) custom-call(bf16[4096,512]{1,0:T(8,128)(2,1)} %refs_0_.5, bf16[4096,512]{1,0:T(8,128)(2,1)} %refs_1_.3, ...), custom_call_target="tpu_custom_call" | custom-call | tf_op jit(solution)/shard_map/totals/pallas_call | solution.py:268
  6.1 3.1 %collective-permute-start.2 = (f32[2,128,128]{2,1,0:T(8,128)S(1)}, f32[2,128,128]{2,1,0:T(8,128)S(1)}, u32[]{:S(2)}, u32[]{:S(2)}) collective-permute-start(f32[2,128,128]{2,1,0:T(8,128)S(1)} %get-tuple-element.16.left_ref), channel_id=1, source_target_pairs={{0,4},{4,0},{8,12},{12,8},{1,5},{5,1},{9,13},{13,9},{2,6},{6,2},{1... | collective-permute-start | bytes 393224 | tf_op jit(solution)/shard_map/ppermute | solution.py:250
  9.3 0.1 collective-permute-start
  9.3 0.0 copy-done
  9.3 1.6 %local.6.refs_0_.refs_3_ = f32[128,4096]{1,0:T(8,128)S(1)} custom-call(bf16[4096,512]{1,0:T(8,128)(2,1)S(1)} %copy-done, bf16[4096,512]{1,0:T(8,128)(2,1)S(1)} %get-tuple-element.12.refs_1_, bf16[4,128,4096]{2,1,0:T(8,128)(2,1)S(1)} %get-tuple-element.13.refs_2_, bf16[4,16,128,128]{3,2,1,0:T(8,128)(2,1)S(1)} %get-tuple-element.14.refs_3_, ...), custom_call_target="tpu_custom_call" | custom-call | tf_op jit(solution)/shard_map/local/pallas_call | solution.py:291
  11.0 1.6 %local.7.refs_0_.refs_2_ = f32[128,4096]{1,0:T(8,128)S(1)} custom-call(bf16[4096,512]{1,0:T(8,128)(2,1)S(1)} %copy-done, bf16[4096,512]{1,0:T(8,128)(2,1)S(1)} %get-tuple-element.12.refs_1_, bf16[4,128,4096]{2,1,0:T(8,128)(2,1)S(1)} %get-tuple-element.13.refs_2_, bf16[4,16,128,128]{3,2,1,0:T(8,128)(2,1)S(1)} %get-tuple-element.14.refs_3_, ...), custom_call_target="tpu_custom_call" | custom-call | tf_op jit(solution)/shard_map/local/pallas_call | solution.py:291
  12.6 1.0 %collective-permute-done.2.right_ref.refs_4_ = f32[2,128,128]{2,1,0:T(8,128)S(1)} collective-permute-done((f32[2,128,128]{2,1,0:T(8,128)S(1)}, f32[2,128,128]{2,1,0:T(8,128)S(1)}, u32[]{:S(2)}, u32[]{:S(2)}) %collective-permute-start.2) | collective-permute-done | bytes 131104 | tf_op jit(solution)/shard_map/ppermute | solution.py:250
  13.6 3.1 %collective-permute-start.3 = (f32[2,128,128]{2,1,0:T(8,128)S(1)}, f32[2,128,128]{2,1,0:T(8,128)S(1)}, u32[]{:S(2)}, u32[]{:S(2)}) collective-permute-start(f32[2,128,128]{2,1,0:T(8,128)S(1)} %join.3), channel_id=1, source_target_pairs={{0,8},{4,12},{8,0},{12,4},{1,9},{5,13},{9,1},{13,5},{2,10},{6,14},... | collective-permute-start | bytes 393224 | tf_op jit(solution)/shard_map/ppermute | solution.py:250
  16.7 0.0 collective-permute-done.refs_5_.right_ref
  16.7 2.6 %collective-permute-start.1 = (f32[2,128,128]{2,1,0:T(8,128)S(1)}, f32[2,128,128]{2,1,0:T(8,128)S(1)}, u32[]{:S(2)}, u32[]{:S(2)}) collective-permute-start(f32[2,128,128]{2,1,0:T(8,128)S(1)} %join.2), channel_id=1, source_target_pairs={{0,8},{4,12},{8,0},{12,4},{1,9},{5,13},{9,1},{13,5},{2,10},{6,14},... | collective-permute-start | bytes 393224 | tf_op jit(solution)/shard_map/ppermute | solution.py:250
  19.3 1.9 %local.4.refs_2_ = f32[128,4096]{1,0:T(8,128)S(1)} custom-call(bf16[4096,512]{1,0:T(8,128)(2,1)S(1)} %copy-done, bf16[4096,512]{1,0:T(8,128)(2,1)S(1)} %get-tuple-element.12.refs_1_, bf16[4,128,4096]{2,1,0:T(8,128)(2,1)S(1)} %get-tuple-element.13.refs_2_, bf16[4,16,128,128]{3,2,1,0:T(8,128)(2,1)S(1)} %get-tuple-element.14.refs_3_, ...), custom_call_target="tpu_custom_call" | custom-call | tf_op jit(solution)/shard_map/local/pallas_call | solution.py:291
  21.2 1.9 %local.5.refs_3_ = f32[128,4096]{1,0:T(8,128)S(1)} custom-call(bf16[4096,512]{1,0:T(8,128)(2,1)S(1)} %copy-done, bf16[4096,512]{1,0:T(8,128)(2,1)S(1)} %get-tuple-element.12.refs_1_, bf16[4,128,4096]{2,1,0:T(8,128)(2,1)S(1)} %get-tuple-element.13.refs_2_, bf16[4,16,128,128]{3,2,1,0:T(8,128)(2,1)S(1)} %get-tuple-element.14.refs_3_, ...), custom_call_target="tpu_custom_call" | custom-call | tf_op jit(solution)/shard_map/local/pallas_call | solution.py:291
  23.1 2.8 %collective-permute-done.3.refs_5_ = f32[2,128,128]{2,1,0:T(8,128)S(1)} collective-permute-done((f32[2,128,128]{2,1,0:T(8,128)S(1)}, f32[2,128,128]{2,1,0:T(8,128)S(1)}, u32[]{:S(2)}, u32[]{:S(2)}) %collective-permute-start.3) | collective-permute-done | bytes 131104 | tf_op jit(solution)/shard_map/ppermute | solution.py:250
  25.9 2.3 %remote.2.refs_5_ = bf16[4096,512]{1,0:T(8,128)(2,1)} custom-call(f32[128,4096]{1,0:T(8,128)S(1)} %get-tuple-element.11.refs_4_.refs_0_, bf16[4096,512]{1,0:T(8,128)(2,1)S(1)} %copy-done, f32[128,4096]{1,0:T(8,128)S(1)} %local.7.refs_0_.refs_2_, f32[128,4096]{1,0:T(8,128)S(1)} %local.6.refs_0_.refs_3_, ...), custom_call_target="tpu_custom_call" | custom-call | tf_op jit(solution)/shard_map/remote/pallas_call | solution.py:319
  28.2 0.0 collective-permute-done.1.refs_4_
  28.2 1.7 %remote.3 = bf16[4096,512]{1,0:T(8,128)(2,1)} custom-call(f32[128,4096]{1,0:T(8,128)S(1)} %get-tuple-element.11.refs_4_.refs_0_, bf16[4096,512]{1,0:T(8,128)(2,1)S(1)} %copy-done, f32[128,4096]{1,0:T(8,128)S(1)} %local.4.refs_2_, f32[128,4096]{1,0:T(8,128)S(1)} %local.5.refs_3_, ...), custom_call_target="tpu_custom_call", output_to_operand_aliasing={{}: (5, {})} | custom-call | tf_op jit(solution)/shard_map/remote/pallas_call | solution.py:319
  (2 shorter events, 0.0 us)
Async XLA Ops:
  0.0 9.3 %copy-start = (bf16[4096,512]{1,0:T(8,128)(2,1)S(1)}, bf16[4096,512]{1,0:T(8,128)(2,1)}, u32[]{:S(2)}) copy-start(bf16[4096,512]{1,0:T(8,128)(2,1)} %refs_1_.5) | copy-start | bytes 12582916
  6.1 7.5 %collective-permute-start.2 = (f32[2,128,128]{2,1,0:T(8,128)S(1)}, f32[2,128,128]{2,1,0:T(8,128)S(1)}, u32[]{:S(2)}, u32[]{:S(2)}) collective-permute-start(f32[2,128,128]{2,1,0:T(8,128)S(1)} %get-tuple-element.16.left_ref), channel_id=1, source_target_pairs={{0,4},{4,0},{8,12},{12,8},{1,5},{5,1},{9,13},{13,9},{2,6},{6,2},{1... | collective-permute-start | bytes 393224 | tf_op jit(solution)/shard_map/ppermute | solution.py:250
  9.3 7.5 %collective-permute-start = (f32[2,128,128]{2,1,0:T(8,128)S(1)}, f32[2,128,128]{2,1,0:T(8,128)S(1)}, u32[]{:S(2)}, u32[]{:S(2)}) collective-permute-start(f32[2,128,128]{2,1,0:T(8,128)S(1)} %get-tuple-element.15.left_ref), channel_id=1, source_target_pairs={{0,4},{4,0},{8,12},{12,8},{1,5},{5,1},{9,13},{13,9},{2,6},{6,2},{1... | collective-permute-start | bytes 393224 | tf_op jit(solution)/shard_map/ppermute | solution.py:250
  13.6 12.3 %collective-permute-start.3 = (f32[2,128,128]{2,1,0:T(8,128)S(1)}, f32[2,128,128]{2,1,0:T(8,128)S(1)}, u32[]{:S(2)}, u32[]{:S(2)}) collective-permute-start(f32[2,128,128]{2,1,0:T(8,128)S(1)} %join.3), channel_id=1, source_target_pairs={{0,8},{4,12},{8,0},{12,4},{1,9},{5,13},{9,1},{13,5},{2,10},{6,14},... | collective-permute-start | bytes 393224 | tf_op jit(solution)/shard_map/ppermute | solution.py:250
  16.7 11.5 %collective-permute-start.1 = (f32[2,128,128]{2,1,0:T(8,128)S(1)}, f32[2,128,128]{2,1,0:T(8,128)S(1)}, u32[]{:S(2)}, u32[]{:S(2)}) collective-permute-start(f32[2,128,128]{2,1,0:T(8,128)S(1)} %join.2), channel_id=1, source_target_pairs={{0,8},{4,12},{8,0},{12,4},{1,9},{5,13},{9,1},{13,5},{2,10},{6,14},... | collective-permute-start | bytes 393224 | tf_op jit(solution)/shard_map/ppermute | solution.py:250

commit v4 on v2

--- a/solution.py
+++ b/solution.py
@@ -245,6 +245,21 @@
     )(total, received, after)
 
 
+def gate_kernel(total_ref, after_ref, out_ref):
+    out_ref[...] = total_ref[...]
+
+
+def gate(total, after):
+    return pl.pallas_call(
+        gate_kernel,
+        in_specs=[VMEM, ANY],
+        out_specs=VMEM,
+        out_shape=jax.ShapeDtypeStruct(total.shape, total.dtype),
+        compiler_params=pltpu.CompilerParams(vmem_limit_bytes=2 * MIB),
+        name="gate",
+    )(total, after)
+
+
 def exchange(total, bit):
     devices = lax.axis_size("ctx")
     return lax.ppermute(total, "ctx", [(device, device ^ 2**bit) for device in range(devices)])
@@ -297,6 +312,7 @@
         name="prepare",
     )(lefts, queries, in_hbm(token_rows[None, :]), in_hbm(jnp.transpose(weight_table, (2, 1, 0))))
 
+    totals[1:] = [gate(total, weights) for total in totals[1:]]
     received = [[exchange(total, 0)] for total in totals]
     parts = []
     after = weights

time: 27.3 us -> 28.1 us (1.029)
  starting transfers between devices: 7.18 us -> 7.99 us
    ppermute x4, starting transfers between devices: 7.18 us -> 7.99 us  [exchange(): lax.ppermute(total, 'ctx', [(device, device ^ 2 ** bit) for device in ran...]
  transfers between devices with their start and end apart: 4 -> 4, of which waited for: 2 -> 2; matrix products, arithmetic and copies ran while one was open for 0% -> 0% of each run, Pallas kernels for 43% -> 42%
where the time goes in v4:
time: 28.1 us; the launch traced here: 27.8 us
  Pallas kernels  17.4 us (62%)
  starting transfers between devices  7.99 us (28%)
  waiting for transfers between devices  2.3 us (8%)
    ppermute x4, starting transfers between devices, exchange(): lax.ppermute(total, 'ctx', [(device, device ^ 2 ** bit) for device in ran...  7.99 us
    pallas_call x4, Pallas kernels, body(): pl.pallas_call(lambda *refs, head=head: local_kernel(head, head % group,...  7.56 us
    pallas_call x1, Pallas kernels, body(): pl.pallas_call(totals_kernel, in_specs=[HBM] * 2, out_specs=[VMEM] * (3 +...  4.19 us
    pallas_call x2, Pallas kernels, body(): pl.pallas_call(lambda *refs, heads=heads: remote_kernel(heads, local_bits...  3.38 us
    ppermute x4, waiting for transfers between devices, exchange(): lax.ppermute(total, 'ctx', [(device, device ^ 2 ** bit) for device in ran...  2.3 us
    pallas_call x1, Pallas kernels, body(): pl.pallas_call(lambda *refs: prepare_kernel(local_bits, *refs), in_specs=...  2.26 us
  transfers between devices with their start and end apart: 4, of which 2 were waited for; matrix products, arithmetic and copies ran while one was open for 0% of the time, Pallas kernels for 42%

profile of v4, /device:TPU:0, one launch (start us, length us, event | category | flops | bytes accessed | tf_op | source)
XLA Modules:
  0.0 27.8 jit_solution(17328207793152041389)
XLA Ops:
  0.0 4.2 %totals.1 = (bf16[4096,512]{1,0:T(8,128)(2,1)S(1)}, bf16[4,128,4096]{2,1,0:T(8,128)(2,1)S(1)}, bf16[4,16,128,128]{3,2,1,0:T(8,128)(2,1)S(1)}, f32[2,128,128]{2,1,0:T(8,128)S(1)}, f32[2,128,128]{2,1,0:T(8,128)S(1)}) custom-call(bf16[4096,512]{1,0:T(8,128)(2,1)} %key_hbm.1, bf16[4096,512]{1,0:T(8,128)(2,1)} %value_hbm.1), custom_call_target="tpu_custom_call" | custom-call | tf_op jit(solution)/shard_map/totals/pallas_call | solution.py:283
  4.2 3.1 %collective-permute-start.1 = (f32[2,128,128]{2,1,0:T(8,128)S(1)}, f32[2,128,128]{2,1,0:T(8,128)S(1)}, u32[]{:S(2)}, u32[]{:S(2)}) collective-permute-start(f32[2,128,128]{2,1,0:T(8,128)S(1)} %get-tuple-element.18.left_ref), channel_id=1, source_target_pairs={{0,4},{4,0},{8,12},{12,8},{1,5},{5,1},{9,13},{13,9},{2,6},{6,2},{1... | collective-permute-start | bytes 393224 | tf_op jit(solution)/shard_map/ppermute | solution.py:265
  7.3 2.3 %prepare.1 = (f32[128,4096]{1,0:T(8,128)S(1)}, bf16[4096,512]{1,0:T(8,128)(2,1)S(1)}) custom-call(bf16[4,16,128,128]{3,2,1,0:T(8,128)(2,1)S(1)} %get-tuple-element.12.refs_0_.refs_3_, bf16[4096,512]{1,0:T(8,128)(2,1)} %refs_1_.1, s32[1,4096]{1,0:T(1,128)} %bitcast.3, f32[21,4,64]{2,1,0:T(4,128)} %bitcast.2), custom_call_target="tpu_custom_call" | custom-call | tf_op jit(solution)/shard_map/prepare/pallas_call | solution.py:301
  9.6 0.1 collective-permute-start
  9.7 1.1 %collective-permute-done.1.refs_5_.right_ref = f32[2,128,128]{2,1,0:T(8,128)S(1)} collective-permute-done((f32[2,128,128]{2,1,0:T(8,128)S(1)}, f32[2,128,128]{2,1,0:T(8,128)S(1)}, u32[]{:S(2)}, u32[]{:S(2)}) %collective-permute-start.1) | collective-permute-done | bytes 131104 | tf_op jit(solution)/shard_map/ppermute | solution.py:265
  10.8 2.8 %collective-permute-start.3 = (f32[2,128,128]{2,1,0:T(8,128)S(1)}, f32[2,128,128]{2,1,0:T(8,128)S(1)}, u32[]{:S(2)}, u32[]{:S(2)}) collective-permute-start(f32[2,128,128]{2,1,0:T(8,128)S(1)} %join.3), channel_id=1, source_target_pairs={{0,8},{4,12},{8,0},{12,4},{1,9},{5,13},{9,1},{13,5},{2,10},{6,14},... | collective-permute-start | bytes 393224 | tf_op jit(solution)/shard_map/ppermute | solution.py:265
  13.7 1.9 %local.6.after_ref.refs_2_ = f32[128,4096]{1,0:T(8,128)S(1)} custom-call(bf16[4096,512]{1,0:T(8,128)(2,1)S(1)} %get-tuple-element.14.refs_0_.refs_1_, bf16[4096,512]{1,0:T(8,128)(2,1)S(1)} %get-tuple-element.15.refs_1_, bf16[4,128,4096]{2,1,0:T(8,128)(2,1)S(1)} %get-tuple-element.16.refs_2_, bf16[4,16,128,128]{3,2,1,0:T(8,128)(2,1)S(1)} %get-tuple-element.12.refs_0_.refs_3_, ...), custom_call_target="tpu_custom_call" | custom-call | tf_op jit(solution)/shard_map/local/pallas_call | solution.py:324
  15.5 1.2 %collective-permute-done.refs_5_.right_ref = f32[2,128,128]{2,1,0:T(8,128)S(1)} collective-permute-done((f32[2,128,128]{2,1,0:T(8,128)S(1)}, f32[2,128,128]{2,1,0:T(8,128)S(1)}, u32[]{:S(2)}, u32[]{:S(2)}) %collective-permute-start) | collective-permute-done | bytes 131104 | tf_op jit(solution)/shard_map/ppermute | solution.py:265
  16.7 2.0 %collective-permute-start.2 = (f32[2,128,128]{2,1,0:T(8,128)S(1)}, f32[2,128,128]{2,1,0:T(8,128)S(1)}, u32[]{:S(2)}, u32[]{:S(2)}) collective-permute-start(f32[2,128,128]{2,1,0:T(8,128)S(1)} %join.2), channel_id=1, source_target_pairs={{0,8},{4,12},{8,0},{12,4},{1,9},{5,13},{9,1},{13,5},{2,10},{6,14},... | collective-permute-start | bytes 393224 | tf_op jit(solution)/shard_map/ppermute | solution.py:265
  18.7 1.9 %local.7.refs_3_ = f32[128,4096]{1,0:T(8,128)S(1)} custom-call(bf16[4096,512]{1,0:T(8,128)(2,1)S(1)} %get-tuple-element.14.refs_0_.refs_1_, bf16[4096,512]{1,0:T(8,128)(2,1)S(1)} %get-tuple-element.15.refs_1_, bf16[4,128,4096]{2,1,0:T(8,128)(2,1)S(1)} %get-tuple-element.16.refs_2_, bf16[4,16,128,128]{3,2,1,0:T(8,128)(2,1)S(1)} %get-tuple-element.12.refs_0_.refs_3_, ...), custom_call_target="tpu_custom_call" | custom-call | tf_op jit(solution)/shard_map/local/pallas_call | solution.py:324
  20.6 1.9 %local.5.refs_3_ = f32[128,4096]{1,0:T(8,128)S(1)} custom-call(bf16[4096,512]{1,0:T(8,128)(2,1)S(1)} %get-tuple-element.14.refs_0_.refs_1_, bf16[4096,512]{1,0:T(8,128)(2,1)S(1)} %get-tuple-element.15.refs_1_, bf16[4,128,4096]{2,1,0:T(8,128)(2,1)S(1)} %get-tuple-element.16.refs_2_, bf16[4,16,128,128]{3,2,1,0:T(8,128)(2,1)S(1)} %get-tuple-element.12.refs_0_.refs_3_, ...), custom_call_target="tpu_custom_call" | custom-call | tf_op jit(solution)/shard_map/local/pallas_call | solution.py:324
  22.5 1.9 %local.4.refs_2_ = f32[128,4096]{1,0:T(8,128)S(1)} custom-call(bf16[4096,512]{1,0:T(8,128)(2,1)S(1)} %get-tuple-element.14.refs_0_.refs_1_, bf16[4096,512]{1,0:T(8,128)(2,1)S(1)} %get-tuple-element.15.refs_1_, bf16[4,128,4096]{2,1,0:T(8,128)(2,1)S(1)} %get-tuple-element.16.refs_2_, bf16[4,16,128,128]{3,2,1,0:T(8,128)(2,1)S(1)} %get-tuple-element.12.refs_0_.refs_3_, ...), custom_call_target="tpu_custom_call" | custom-call | tf_op jit(solution)/shard_map/local/pallas_call | solution.py:324
  24.4 0.0 collective-permute-done.3.refs_4_
  24.4 1.7 %remote.2.refs_5_ = bf16[4096,512]{1,0:T(8,128)(2,1)} custom-call(f32[128,4096]{1,0:T(8,128)S(1)} %get-tuple-element.13.after_ref.refs_4_.refs_0_, bf16[4096,512]{1,0:T(8,128)(2,1)S(1)} %get-tuple-element.14.refs_0_.refs_1_, f32[128,4096]{1,0:T(8,128)S(1)} %local.6.after_ref.refs_2_, f32[128,4096]{1,0:T(8,128)S(1)} %local.7.refs_3_, ...), custom_call_target="tpu_custom_call" | custom-call | tf_op jit(solution)/shard_map/remote/pallas_call | solution.py:339
  26.1 0.0 collective-permute-done.2.refs_4_
  26.1 1.7 %remote.3 = bf16[4096,512]{1,0:T(8,128)(2,1)} custom-call(f32[128,4096]{1,0:T(8,128)S(1)} %get-tuple-element.13.after_ref.refs_4_.refs_0_, bf16[4096,512]{1,0:T(8,128)(2,1)S(1)} %get-tuple-element.14.refs_0_.refs_1_, f32[128,4096]{1,0:T(8,128)S(1)} %local.4.refs_2_, f32[128,4096]{1,0:T(8,128)S(1)} %local.5.refs_3_, ...), custom_call_target="tpu_custom_call", output_to_operand_aliasing={{}: (5, {})} | custom-call | tf_op jit(solution)/shard_map/remote/pallas_call | solution.py:339
  (3 shorter events, 0.0 us)
Async XLA Ops:
  4.2 6.6 %collective-permute-start.1 = (f32[2,128,128]{2,1,0:T(8,128)S(1)}, f32[2,128,128]{2,1,0:T(8,128)S(1)}, u32[]{:S(2)}, u32[]{:S(2)}) collective-permute-start(f32[2,128,128]{2,1,0:T(8,128)S(1)} %get-tuple-element.18.left_ref), channel_id=1, source_target_pairs={{0,4},{4,0},{8,12},{12,8},{1,5},{5,1},{9,13},{13,9},{2,6},{6,2},{1... | collective-permute-start | bytes 393224 | tf_op jit(solution)/shard_map/ppermute | solution.py:265
  9.6 7.1 %collective-permute-start = (f32[2,128,128]{2,1,0:T(8,128)S(1)}, f32[2,128,128]{2,1,0:T(8,128)S(1)}, u32[]{:S(2)}, u32[]{:S(2)}) collective-permute-start(f32[2,128,128]{2,1,0:T(8,128)S(1)} %gate.1.left_ref), channel_id=1, source_target_pairs={{0,4},{4,0},{8,12},{12,8},{1,5},{5,1},{9,13},{13,9},{2,6},{6,2},{1... | collective-permute-start | bytes 393224 | tf_op jit(solution)/shard_map/ppermute | solution.py:265
  10.8 13.6 %collective-permute-start.3 = (f32[2,128,128]{2,1,0:T(8,128)S(1)}, f32[2,128,128]{2,1,0:T(8,128)S(1)}, u32[]{:S(2)}, u32[]{:S(2)}) collective-permute-start(f32[2,128,128]{2,1,0:T(8,128)S(1)} %join.3), channel_id=1, source_target_pairs={{0,8},{4,12},{8,0},{12,4},{1,9},{5,13},{9,1},{13,5},{2,10},{6,14},... | collective-permute-start | bytes 393224 | tf_op jit(solution)/shard_map/ppermute | solution.py:265
  16.7 9.4 %collective-permute-start.2 = (f32[2,128,128]{2,1,0:T(8,128)S(1)}, f32[2,128,128]{2,1,0:T(8,128)S(1)}, u32[]{:S(2)}, u32[]{:S(2)}) collective-permute-start(f32[2,128,128]{2,1,0:T(8,128)S(1)} %join.2), channel_id=1, source_target_pairs={{0,8},{4,12},{8,0},{12,4},{1,9},{5,13},{9,1},{13,5},{2,10},{6,14},... | collective-permute-start | bytes 393224 | tf_op jit(solution)/shard_map/ppermute | solution.py:265

commit v5 on v2

--- a/solution.py
+++ b/solution.py
@@ -4,6 +4,7 @@
 from jax.experimental import pallas as pl
 from jax.experimental.pallas import tpu as pltpu
 from jax.sharding import PartitionSpec as P
+
 
 BLOCK = 256
 HALF = BLOCK // 2
@@ -14,7 +15,7 @@
 LANES = 128
 SLOT = 32
 PIECES = 8
-GROUPS = 2
+DEPTH = 3
 MIB = 1 << 20
 VMEM = pl.BlockSpec(memory_space=pltpu.VMEM)
 HBM = pl.BlockSpec(memory_space=pltpu.HBM)
@@ -47,19 +48,19 @@
         ) + jnp.dot(low, pick, preferred_element_type=jnp.float32)
 
 
-def pipelined(units, begin, finish):
-    ahead = begin(units[0])
-    for unit, following in zip(units, units[1:] + [None]):
-        held, ahead = ahead, None if following is None else begin(following)
-        finish(unit, held)
-
-
-def totals_kernel(key_hbm, value_hbm, key_ref, turned_ref, left_ref, *refs):
-    total_refs = refs[:GROUPS]
-    value_ref, sems = refs[GROUPS:]
+def pipelined(units, begin, finish, depth=1):
+    begun = [begin(unit) for unit in units[:depth]]
+    for index, unit in enumerate(units):
+        if index + depth < len(units):
+            begun.append(begin(units[index + depth]))
+        finish(unit, begun[index])
+
+
+def totals_kernel(home, key_hbm, value_hbm, key_ref, turned_ref, left_ref, *refs):
+    total_refs = refs[:-2]
+    value_ref, sems = refs[-2:]
     token_count = key_ref.shape[0]
     head_count = turned_ref.shape[0]
-    group = head_count // GROUPS
     block_count = token_count // BLOCK
     size = token_count // PIECES
     blocks = block_count // PIECES
@@ -97,7 +98,7 @@
         if block + 1 < block_count:
             left_ref[head, block] = carry.astype(jnp.bfloat16)
         else:
-            total_refs[head // group][head % group] = carry
+            total_refs[home[head][0]][home[head][1]] = carry
 
     for piece, pair in enumerate(copies):
         for copy in pair:
@@ -190,18 +191,18 @@
             preferred_element_type=jnp.float32,
         )
 
-    pipelined(list(range(block_count)), begin, finish)
-
-
-def remote_kernel(heads, level, *refs):
+    pipelined(list(range(block_count)), begin, finish, DEPTH)
+
+
+def remote_kernel(heads, places, level, *refs):
     count = len(heads)
     weight_ref, query_ref = refs[:2]
     part_refs = refs[2 : 2 + count]
-    state_ref = refs[2 + count]
+    state_refs = refs[2 + count : 2 + 2 * count]
     out_hbm, buffer, sems = refs[-3:]
     token_count = weight_ref.shape[1]
     size = token_count // PIECES
-    states = [state_ref[place].astype(jnp.bfloat16) for place in range(count)]
+    states = [ref[place].astype(jnp.bfloat16) for ref, place in zip(state_refs, places)]
     copies = []
 
     def begin(unit):
@@ -247,7 +248,14 @@
 
 def exchange(total, bit):
     devices = lax.axis_size("ctx")
-    return lax.ppermute(total, "ctx", [(device, device ^ 2**bit) for device in range(devices)])
+    pairs = [(device, device ^ 2**bit) for device in range(devices)]
+    return lax.ppermute(total, "ctx", pairs)
+
+
+def groups_of(head_count):
+    half = head_count // 2
+    firsts = sorted({0, half // 2, half})
+    return [range(first, last) for first, last in zip(firsts, firsts[1:] + [head_count])]
 
 
 def body(queries, key_vectors, value_vectors, token_rows, weight_table):
@@ -258,7 +266,9 @@
     local_bits = token_count.bit_length() - 1
     devices = lax.axis_size("ctx")
     bit_count = devices.bit_length() - 1
-    group = head_count // GROUPS
+    half = head_count // 2
+    groups = groups_of(head_count)
+    home = {head: (index, head - heads[0]) for index, heads in enumerate(groups) for head in heads}
     shape = jax.ShapeDtypeStruct
     whole = shape(queries.shape, queries.dtype)
     params = pltpu.CompilerParams(vmem_limit_bytes=8 * MIB)
@@ -266,14 +276,14 @@
     queries, key_vectors, value_vectors = in_hbm(queries), in_hbm(key_vectors), in_hbm(value_vectors)
 
     keys, turned, lefts, *totals = pl.pallas_call(
-        totals_kernel,
+        lambda *refs: totals_kernel(home, *refs),
         in_specs=[HBM] * 2,
-        out_specs=[VMEM] * (3 + GROUPS),
+        out_specs=[VMEM] * (3 + len(groups)),
         out_shape=[
             whole,
             shape((head_count, width, token_count), jnp.bfloat16),
             shape((head_count, block_count, width, width), jnp.bfloat16),
-            *[shape((group, width, width), jnp.float32)] * GROUPS,
+            *[shape((len(heads), width, width), jnp.float32) for heads in groups],
         ],
         scratch_shapes=[
             pltpu.VMEM(queries.shape, queries.dtype),
@@ -301,33 +311,37 @@
     parts = []
     after = weights
     for index, total in enumerate(totals):
+        if index == len(groups) - 1:
+            after = parts[0]
         for bit in range(1, bit_count):
             total = join(total, received[index][-1], after)
             received[index].append(exchange(total, bit))
-        for head in range(index * group, (index + 1) * group):
-            parts += pl.pallas_call(
-                lambda *refs, head=head: local_kernel(head, head % group, local_bits, *refs),
+        for head in groups[index]:
+            local = pl.pallas_call(
+                lambda *refs, head=head: local_kernel(head, home[head][1], local_bits, *refs),
                 in_specs=[VMEM] * (5 + bit_count - 1),
                 out_specs=[VMEM],
                 out_shape=[shape((width, token_count), jnp.float32)],
                 scratch_shapes=[pltpu.VMEM((2 * block_count, TILES, HALF), jnp.float32)],
                 compiler_params=params,
                 name="local",
-            )(query, keys, turned, lefts, weights, *received[index][:-1])
-        after = parts[0]
+            )
+            parts += local(query, keys, turned, lefts, weights, *received[index][:-1])
 
     out = None
-    for index, arrived in enumerate(received):
-        heads = tuple(range(index * group, (index + 1) * group))
-        operands = [weights, query] + [parts[head] for head in heads] + [arrived[-1]]
+    for first in range(0, head_count, half):
+        heads = tuple(range(first, first + half))
+        places = tuple(home[head][1] for head in heads)
+        operands = [weights, query] + [parts[head] for head in heads]
+        operands += [received[home[head][0]][-1] for head in heads]
         out = pl.pallas_call(
-            lambda *refs, heads=heads: remote_kernel(heads, local_bits + bit_count, *refs),
+            lambda *refs, heads=heads, places=places: remote_kernel(heads, places, local_bits + bit_count, *refs),
             in_specs=[VMEM] * len(operands) + ([] if out is None else [HBM]),
             out_specs=HBM,
             out_shape=whole,
             input_output_aliases={} if out is None else {len(operands): 0},
             scratch_shapes=[
-                pltpu.VMEM((token_count, group * width), jnp.bfloat16),
+                pltpu.VMEM((token_count, half * width), jnp.bfloat16),
                 pltpu.SemaphoreType.DMA((PIECES,)),
             ],
             compiler_params=params,
@@ -344,6 +358,5 @@
         P(("groups", "ctx")),
         P(None, "head", None),
     )
-    return jax.shard_map(
-        body, mesh=mesh, in_specs=placed, out_specs=P(("groups", "ctx"), "head"), check_vma=False
-    )
+
+    return jax.shard_map(body, mesh=mesh, in_specs=placed, out_specs=P(("groups", "ctx"), "head"), check_vma=False)

time: 27.3 us -> 31.6 us (1.16)
  starting transfers between devices: 7.18 us -> 11 us
  waiting for transfers between devices: 2.35 us -> 3.91 us
  Pallas kernels: 17.4 us -> 16.3 us
    ppermute x4 -> x6, starting transfers between devices: 7.18 us -> 11 us  [exchange(): return lax.ppermute(total, 'ctx', pairs)]
    ppermute x4 -> x6, waiting for transfers between devices: 2.35 us -> 3.91 us  [exchange(): return lax.ppermute(total, 'ctx', pairs)]
    pallas_call x7, Pallas kernels: 15.1 us -> 14 us  [the longest x4 6.46 us: body(): parts += local(query, keys, turned, lefts, weights, *received[index][:-1])]
  transfers between devices with their start and end apart: 4 -> 6, of which waited for: 2 -> 3; matrix products, arithmetic and copies ran while one was open for 0% -> 0% of each run, Pallas kernels for 43% -> 33%
where the time goes in v5:
time: 31.6 us; the launch traced here: 31.3 us
  Pallas kernels  16.3 us (52%)
  starting transfers between devices  11 us (35%)
  waiting for transfers between devices  3.91 us (12%)
    ppermute x6, starting transfers between devices, exchange(): return lax.ppermute(total, 'ctx', pairs)  11 us
    pallas_call x4, Pallas kernels, body(): parts += local(query, keys, turned, lefts, weights, *received[index][:-1])  6.46 us
    pallas_call x1, Pallas kernels, body(): pl.pallas_call(lambda *refs: totals_kernel(home, *refs), in_specs=[HBM] *...  4.19 us
    ppermute x6, waiting for transfers between devices, exchange(): return lax.ppermute(total, 'ctx', pairs)  3.91 us
    pallas_call x2, Pallas kernels, body(): pl.pallas_call(lambda *refs, heads=heads, places=places: remote_kernel(he...  3.37 us
    pallas_call x1, Pallas kernels, body(): pl.pallas_call(lambda *refs: prepare_kernel(local_bits, *refs), in_specs=...  2.26 us
  transfers between devices with their start and end apart: 6, of which 3 were waited for; matrix products, arithmetic and copies ran while one was open for 0% of the time, Pallas kernels for 33%

profile of v5, /device:TPU:0, one launch (start us, length us, event | category | flops | bytes accessed | tf_op | source)
XLA Modules:
  0.0 31.3 jit_solution(10449598586226854524)
XLA Ops:
  0.0 4.2 %totals.1 = (bf16[4096,512]{1,0:T(8,128)(2,1)S(1)}, bf16[4,128,4096]{2,1,0:T(8,128)(2,1)S(1)}, bf16[4,16,128,128]{3,2,1,0:T(8,128)(2,1)S(1)}, f32[1,128,128]{2,1...) custom-call(bf16[4096,512]{1,0:T(8,128)(2,1)} %refs_0_.1, bf16[4096,512]{1,0:T(8,128)(2,1)} %refs_1_.2), custom_call_target="tpu_custom_call" | custom-call | tf_op jit(solution)/shard_map/totals/pallas_call | solution.py:278
  4.2 3.1 %collective-permute-start = (f32[2,128,128]{2,1,0:T(8,128)S(1)}, f32[2,128,128]{2,1,0:T(8,128)S(1)}, u32[]{:S(2)}, u32[]{:S(2)}) collective-permute-start(f32[2,128,128]{2,1,0:T(8,128)S(1)} %get-tuple-element.18.left_ref), channel_id=1, source_target_pairs={{0,4},{4,0},{8,12},{12,8},{1,5},{5,1},{9,13},{13,9},{2,6},{6,2},{1... | collective-permute-start | bytes 393224 | tf_op jit(solution)/shard_map/ppermute | solution.py:252
  7.3 0.1 collective-permute-start.1
  7.4 1.9 %collective-permute-start.3 = (f32[1,128,128]{2,1,0:T(8,128)S(1)}, f32[1,128,128]{2,1,0:T(8,128)S(1)}, u32[]{:S(2)}, u32[]{:S(2)}) collective-permute-start(f32[1,128,128]{2,1,0:T(8,128)S(1)} %get-tuple-element.20.left_ref), channel_id=1, source_target_pairs={{0,4},{4,0},{8,12},{12,8},{1,5},{5,1},{9,13},{13,9},{2,6},{6,2},{1... | collective-permute-start | bytes 196616 | tf_op jit(solution)/shard_map/ppermute | solution.py:252
  9.3 2.3 %prepare.1 = (f32[128,4096]{1,0:T(8,128)S(1)}, bf16[4096,512]{1,0:T(8,128)(2,1)S(1)}) custom-call(bf16[4,16,128,128]{3,2,1,0:T(8,128)(2,1)S(1)} %get-tuple-element.13.refs_0_.refs_3_, bf16[4096,512]{1,0:T(8,128)(2,1)} %refs_1_.3, s32[1,4096]{1,0:T(1,128)} %bitcast.3, f32[21,4,64]{2,1,0:T(4,128)} %bitcast.2), custom_call_target="tpu_custom_call" | custom-call | tf_op jit(solution)/shard_map/prepare/pallas_call | solution.py:296
  11.6 1.3 %collective-permute-done.1.refs_5_.right_ref = f32[1,128,128]{2,1,0:T(8,128)S(1)} collective-permute-done((f32[1,128,128]{2,1,0:T(8,128)S(1)}, f32[1,128,128]{2,1,0:T(8,128)S(1)}, u32[]{:S(2)}, u32[]{:S(2)}) %collective-permute-start.1) | collective-permute-done | bytes 65568 | tf_op jit(solution)/shard_map/ppermute | solution.py:252
  12.9 1.6 %local.6.after_ref.refs_2_ = f32[128,4096]{1,0:T(8,128)S(1)} custom-call(bf16[4096,512]{1,0:T(8,128)(2,1)S(1)} %get-tuple-element.15.refs_0_.refs_1_, bf16[4096,512]{1,0:T(8,128)(2,1)S(1)} %get-tuple-element.16.refs_1_, bf16[4,128,4096]{2,1,0:T(8,128)(2,1)S(1)} %get-tuple-element.17.refs_2_, bf16[4,16,128,128]{3,2,1,0:T(8,128)(2,1)S(1)} %get-tuple-element.13.refs_0_.refs_3_, ...), custom_call_target="tpu_custom_call" | custom-call | tf_op jit(solution)/shard_map/local/pallas_call | solution.py:329
  14.5 0.0 collective-permute-done.refs_5_.right_ref
  14.6 2.8 %collective-permute-start.2 = (f32[2,128,128]{2,1,0:T(8,128)S(1)}, f32[2,128,128]{2,1,0:T(8,128)S(1)}, u32[]{:S(2)}, u32[]{:S(2)}) collective-permute-start(f32[2,128,128]{2,1,0:T(8,128)S(1)} %join.3), channel_id=1, source_target_pairs={{0,8},{4,12},{8,0},{12,4},{1,9},{5,13},{9,1},{13,5},{2,10},{6,14},... | collective-permute-start | bytes 393224 | tf_op jit(solution)/shard_map/ppermute | solution.py:252
  17.4 0.0 collective-permute-done.3.refs_5_.right_ref
  17.4 0.2 collective-permute-start.5
  17.7 2.8 %collective-permute-start.4 = (f32[1,128,128]{2,1,0:T(8,128)S(1)}, f32[1,128,128]{2,1,0:T(8,128)S(1)}, u32[]{:S(2)}, u32[]{:S(2)}) collective-permute-start(f32[1,128,128]{2,1,0:T(8,128)S(1)} %join.4), channel_id=1, source_target_pairs={{0,8},{4,12},{8,0},{12,4},{1,9},{5,13},{9,1},{13,5},{2,10},{6,14},... | collective-permute-start | bytes 196616 | tf_op jit(solution)/shard_map/ppermute | solution.py:252
  20.5 1.6 %local.7.refs_3_ = f32[128,4096]{1,0:T(8,128)S(1)} custom-call(bf16[4096,512]{1,0:T(8,128)(2,1)S(1)} %get-tuple-element.15.refs_0_.refs_1_, bf16[4096,512]{1,0:T(8,128)(2,1)S(1)} %get-tuple-element.16.refs_1_, bf16[4,128,4096]{2,1,0:T(8,128)(2,1)S(1)} %get-tuple-element.17.refs_2_, bf16[4,16,128,128]{3,2,1,0:T(8,128)(2,1)S(1)} %get-tuple-element.13.refs_0_.refs_3_, ...), custom_call_target="tpu_custom_call" | custom-call | tf_op jit(solution)/shard_map/local/pallas_call | solution.py:329
  22.1 1.6 %local.5.refs_3_ = f32[128,4096]{1,0:T(8,128)S(1)} custom-call(bf16[4096,512]{1,0:T(8,128)(2,1)S(1)} %get-tuple-element.15.refs_0_.refs_1_, bf16[4096,512]{1,0:T(8,128)(2,1)S(1)} %get-tuple-element.16.refs_1_, bf16[4,128,4096]{2,1,0:T(8,128)(2,1)S(1)} %get-tuple-element.17.refs_2_, bf16[4,16,128,128]{3,2,1,0:T(8,128)(2,1)S(1)} %get-tuple-element.13.refs_0_.refs_3_, ...), custom_call_target="tpu_custom_call" | custom-call | tf_op jit(solution)/shard_map/local/pallas_call | solution.py:329
  23.7 1.6 %local.4.refs_2_ = f32[128,4096]{1,0:T(8,128)S(1)} custom-call(bf16[4096,512]{1,0:T(8,128)(2,1)S(1)} %get-tuple-element.15.refs_0_.refs_1_, bf16[4096,512]{1,0:T(8,128)(2,1)S(1)} %get-tuple-element.16.refs_1_, bf16[4,128,4096]{2,1,0:T(8,128)(2,1)S(1)} %get-tuple-element.17.refs_2_, bf16[4,16,128,128]{3,2,1,0:T(8,128)(2,1)S(1)} %get-tuple-element.13.refs_0_.refs_3_, ...), custom_call_target="tpu_custom_call" | custom-call | tf_op jit(solution)/shard_map/local/pallas_call | solution.py:329
  25.3 1.9 %collective-permute-done.5.refs_5_ = f32[1,128,128]{2,1,0:T(8,128)S(1)} collective-permute-done((f32[1,128,128]{2,1,0:T(8,128)S(1)}, f32[1,128,128]{2,1,0:T(8,128)S(1)}, u32[]{:S(2)}, u32[]{:S(2)}) %collective-permute-start.5) | collective-permute-done | bytes 65568 | tf_op jit(solution)/shard_map/ppermute | solution.py:252
  27.2 0.7 %collective-permute-done.4.refs_4_ = f32[1,128,128]{2,1,0:T(8,128)S(1)} collective-permute-done((f32[1,128,128]{2,1,0:T(8,128)S(1)}, f32[1,128,128]{2,1,0:T(8,128)S(1)}, u32[]{:S(2)}, u32[]{:S(2)}) %collective-permute-start.4) | collective-permute-done | bytes 65568 | tf_op jit(solution)/shard_map/ppermute | solution.py:252
  27.9 1.7 %remote.2.refs_6_ = bf16[4096,512]{1,0:T(8,128)(2,1)} custom-call(f32[128,4096]{1,0:T(8,128)S(1)} %get-tuple-element.14.refs_4_.after_ref.refs_0_, bf16[4096,512]{1,0:T(8,128)(2,1)S(1)} %get-tuple-element.15.refs_0_.refs_1_, f32[128,4096]{1,0:T(8,128)S(1)} %local.6.after_ref.refs_2_, f32[128,4096]{1,0:T(8,128)S(1)} %local.7.refs_3_, ...), custom_call_target="tpu_custom_call" | custom-call | tf_op jit(solution)/shard_map/remote/pallas_call | solution.py:337
  29.6 0.0 collective-permute-done.2.refs_4_.refs_5_
  29.6 1.7 %remote.3 = bf16[4096,512]{1,0:T(8,128)(2,1)} custom-call(f32[128,4096]{1,0:T(8,128)S(1)} %get-tuple-element.14.refs_4_.after_ref.refs_0_, bf16[4096,512]{1,0:T(8,128)(2,1)S(1)} %get-tuple-element.15.refs_0_.refs_1_, f32[128,4096]{1,0:T(8,128)S(1)} %local.4.refs_2_, f32[128,4096]{1,0:T(8,128)S(1)} %local.5.refs_3_, ...), custom_call_target="tpu_custom_call", output_to_operand_aliasing={{}: (6, {})} | custom-call | tf_op jit(solution)/shard_map/remote/pallas_call | solution.py:337
  (3 shorter events, 0.0 us)
Async XLA Ops:
  4.2 10.3 %collective-permute-start = (f32[2,128,128]{2,1,0:T(8,128)S(1)}, f32[2,128,128]{2,1,0:T(8,128)S(1)}, u32[]{:S(2)}, u32[]{:S(2)}) collective-permute-start(f32[2,128,128]{2,1,0:T(8,128)S(1)} %get-tuple-element.18.left_ref), channel_id=1, source_target_pairs={{0,4},{4,0},{8,12},{12,8},{1,5},{5,1},{9,13},{13,9},{2,6},{6,2},{1... | collective-permute-start | bytes 393224 | tf_op jit(solution)/shard_map/ppermute | solution.py:252
  7.3 5.6 %collective-permute-start.1 = (f32[1,128,128]{2,1,0:T(8,128)S(1)}, f32[1,128,128]{2,1,0:T(8,128)S(1)}, u32[]{:S(2)}, u32[]{:S(2)}) collective-permute-start(f32[1,128,128]{2,1,0:T(8,128)S(1)} %get-tuple-element.19.left_ref), channel_id=1, source_target_pairs={{0,4},{4,0},{8,12},{12,8},{1,5},{5,1},{9,13},{13,9},{2,6},{6,2},{1... | collective-permute-start | bytes 196616 | tf_op jit(solution)/shard_map/ppermute | solution.py:252
  7.4 10.0 %collective-permute-start.3 = (f32[1,128,128]{2,1,0:T(8,128)S(1)}, f32[1,128,128]{2,1,0:T(8,128)S(1)}, u32[]{:S(2)}, u32[]{:S(2)}) collective-permute-start(f32[1,128,128]{2,1,0:T(8,128)S(1)} %get-tuple-element.20.left_ref), channel_id=1, source_target_pairs={{0,4},{4,0},{8,12},{12,8},{1,5},{5,1},{9,13},{13,9},{2,6},{6,2},{1... | collective-permute-start | bytes 196616 | tf_op jit(solution)/shard_map/ppermute | solution.py:252
  14.6 15.0 %collective-permute-start.2 = (f32[2,128,128]{2,1,0:T(8,128)S(1)}, f32[2,128,128]{2,1,0:T(8,128)S(1)}, u32[]{:S(2)}, u32[]{:S(2)}) collective-permute-start(f32[2,128,128]{2,1,0:T(8,128)S(1)} %join.3), channel_id=1, source_target_pairs={{0,8},{4,12},{8,0},{12,4},{1,9},{5,13},{9,1},{13,5},{2,10},{6,14},... | collective-permute-start | bytes 393224 | tf_op jit(solution)/shard_map/ppermute | solution.py:252
  17.4 9.8 %collective-permute-start.5 = (f32[1,128,128]{2,1,0:T(8,128)S(1)}, f32[1,128,128]{2,1,0:T(8,128)S(1)}, u32[]{:S(2)}, u32[]{:S(2)}) collective-permute-start(f32[1,128,128]{2,1,0:T(8,128)S(1)} %join.5), channel_id=1, source_target_pairs={{0,8},{4,12},{8,0},{12,4},{1,9},{5,13},{9,1},{13,5},{2,10},{6,14},... | collective-permute-start | bytes 196616 | tf_op jit(solution)/shard_map/ppermute | solution.py:252
  17.7 10.3 %collective-permute-start.4 = (f32[1,128,128]{2,1,0:T(8,128)S(1)}, f32[1,128,128]{2,1,0:T(8,128)S(1)}, u32[]{:S(2)}, u32[]{:S(2)}) collective-permute-start(f32[1,128,128]{2,1,0:T(8,128)S(1)} %join.4), channel_id=1, source_target_pairs={{0,8},{4,12},{8,0},{12,4},{1,9},{5,13},{9,1},{13,5},{2,10},{6,14},... | collective-permute-start | bytes 196616 | tf_op jit(solution)/shard_map/ppermute | solution.py:252

commit v6 on v2

--- a/solution.py
+++ b/solution.py
@@ -15,6 +15,7 @@
 SLOT = 32
 PIECES = 8
 GROUPS = 2
+DEPTH = 3
 MIB = 1 << 20
 VMEM = pl.BlockSpec(memory_space=pltpu.VMEM)
 HBM = pl.BlockSpec(memory_space=pltpu.HBM)
@@ -47,11 +48,12 @@
         ) + jnp.dot(low, pick, preferred_element_type=jnp.float32)
 
 
-def pipelined(units, begin, finish):
-    ahead = begin(units[0])
-    for unit, following in zip(units, units[1:] + [None]):
-        held, ahead = ahead, None if following is None else begin(following)
-        finish(unit, held)
+def pipelined(units, begin, finish, depth=1):
+    begun = [begin(unit) for unit in units[:depth]]
+    for index, unit in enumerate(units):
+        if index + depth < len(units):
+            begun.append(begin(units[index + depth]))
+        finish(unit, begun[index])
 
 
 def totals_kernel(key_hbm, value_hbm, key_ref, turned_ref, left_ref, *refs):
@@ -190,7 +192,7 @@
             preferred_element_type=jnp.float32,
         )
 
-    pipelined(list(range(block_count)), begin, finish)
+    pipelined(list(range(block_count)), begin, finish, DEPTH)
 
 
 def remote_kernel(heads, level, *refs):

time: 27.3 us -> 27.3 us (level)
  Pallas kernels: 17.4 us -> 16.3 us
  waiting for transfers between devices: 2.35 us -> 3.18 us
    pallas_call x4, Pallas kernels: 7.56 us -> 6.46 us  [body(): pl.pallas_call(lambda *refs, head=head: local_kernel(head, head % group,...]
    ppermute x4, waiting for transfers between devices: 2.35 us -> 3.18 us  [exchange(): lax.ppermute(total, 'ctx', [(device, device ^ 2 ** bit) for device in ran...]
  transfers between devices with their start and end apart: 4 -> 4, of which waited for: 2 -> 2; matrix products, arithmetic and copies ran while one was open for 0% -> 0% of each run, Pallas kernels for 43% -> 39%
where the time goes in v6:
time: 27.3 us; the launch traced here: 27 us
  Pallas kernels  16.3 us (60%)
  starting transfers between devices  7.45 us (27%)
  waiting for transfers between devices  3.18 us (12%)
    ppermute x4, starting transfers between devices, exchange(): lax.ppermute(total, 'ctx', [(device, device ^ 2 ** bit) for device in ran...  7.45 us
    pallas_call x4, Pallas kernels, body(): pl.pallas_call(lambda *refs, head=head: local_kernel(head, head % group,...  6.46 us
    pallas_call x1, Pallas kernels, body(): pl.pallas_call(totals_kernel, in_specs=[HBM] * 2, out_specs=[VMEM] * (3 +...  4.19 us
    pallas_call x2, Pallas kernels, body(): pl.pallas_call(lambda *refs, heads=heads: remote_kernel(heads, local_bits...  3.37 us
    ppermute x4, waiting for transfers between devices, exchange(): lax.ppermute(total, 'ctx', [(device, device ^ 2 ** bit) for device in ran...  3.18 us
    pallas_call x1, Pallas kernels, body(): pl.pallas_call(lambda *refs: prepare_kernel(local_bits, *refs), in_specs=...  2.26 us
  transfers between devices with their start and end apart: 4, of which 2 were waited for; matrix products, arithmetic and copies ran while one was open for 0% of the time, Pallas kernels for 39%

profile of v6, /device:TPU:0, one launch (start us, length us, event | category | flops | bytes accessed | tf_op | source)
XLA Modules:
  0.0 27.0 jit_solution(17307475451976727118)
XLA Ops:
  0.0 4.2 %totals.1 = (bf16[4096,512]{1,0:T(8,128)(2,1)S(1)}, bf16[4,128,4096]{2,1,0:T(8,128)(2,1)S(1)}, bf16[4,16,128,128]{3,2,1,0:T(8,128)(2,1)S(1)}, f32[2,128,128]{2,1,0:T(8,128)S(1)}, f32[2,128,128]{2,1,0:T(8,128)S(1)}) custom-call(bf16[4096,512]{1,0:T(8,128)(2,1)} %key_hbm.1, bf16[4096,512]{1,0:T(8,128)(2,1)} %value_hbm.1), custom_call_target="tpu_custom_call" | custom-call | tf_op jit(solution)/shard_map/totals/pallas_call | solution.py:270
  4.2 3.1 %collective-permute-start.1 = (f32[2,128,128]{2,1,0:T(8,128)S(1)}, f32[2,128,128]{2,1,0:T(8,128)S(1)}, u32[]{:S(2)}, u32[]{:S(2)}) collective-permute-start(f32[2,128,128]{2,1,0:T(8,128)S(1)} %get-tuple-element.18.left_ref), channel_id=1, source_target_pairs={{0,4},{4,0},{8,12},{12,8},{1,5},{5,1},{9,13},{13,9},{2,6},{6,2},{1... | collective-permute-start | bytes 393224 | tf_op jit(solution)/shard_map/ppermute | solution.py:252
  7.3 0.1 collective-permute-start
  7.4 2.3 %prepare.1 = (f32[128,4096]{1,0:T(8,128)S(1)}, bf16[4096,512]{1,0:T(8,128)(2,1)S(1)}) custom-call(bf16[4,16,128,128]{3,2,1,0:T(8,128)(2,1)S(1)} %get-tuple-element.12.refs_0_.refs_3_, bf16[4096,512]{1,0:T(8,128)(2,1)} %refs_1_.1, s32[1,4096]{1,0:T(1,128)} %bitcast.3, f32[21,4,64]{2,1,0:T(4,128)} %bitcast.2), custom_call_target="tpu_custom_call" | custom-call | tf_op jit(solution)/shard_map/prepare/pallas_call | solution.py:288
  9.7 2.0 %collective-permute-done.1.refs_5_.right_ref = f32[2,128,128]{2,1,0:T(8,128)S(1)} collective-permute-done((f32[2,128,128]{2,1,0:T(8,128)S(1)}, f32[2,128,128]{2,1,0:T(8,128)S(1)}, u32[]{:S(2)}, u32[]{:S(2)}) %collective-permute-start.1) | collective-permute-done | bytes 131104 | tf_op jit(solution)/shard_map/ppermute | solution.py:252
  11.7 3.1 %collective-permute-start.3 = (f32[2,128,128]{2,1,0:T(8,128)S(1)}, f32[2,128,128]{2,1,0:T(8,128)S(1)}, u32[]{:S(2)}, u32[]{:S(2)}) collective-permute-start(f32[2,128,128]{2,1,0:T(8,128)S(1)} %join.3), channel_id=1, source_target_pairs={{0,8},{4,12},{8,0},{12,4},{1,9},{5,13},{9,1},{13,5},{2,10},{6,14},... | collective-permute-start | bytes 393224 | tf_op jit(solution)/shard_map/ppermute | solution.py:252
  14.8 1.6 %local.6.after_ref.refs_2_ = f32[128,4096]{1,0:T(8,128)S(1)} custom-call(bf16[4096,512]{1,0:T(8,128)(2,1)S(1)} %get-tuple-element.14.refs_0_.refs_1_, bf16[4096,512]{1,0:T(8,128)(2,1)S(1)} %get-tuple-element.15.refs_1_, bf16[4,128,4096]{2,1,0:T(8,128)(2,1)S(1)} %get-tuple-element.16.refs_2_, bf16[4,16,128,128]{3,2,1,0:T(8,128)(2,1)S(1)} %get-tuple-element.12.refs_0_.refs_3_, ...), custom_call_target="tpu_custom_call" | custom-call | tf_op jit(solution)/shard_map/local/pallas_call | solution.py:310
  16.4 0.0 collective-permute-done.refs_5_.right_ref
  16.4 1.1 %collective-permute-start.2 = (f32[2,128,128]{2,1,0:T(8,128)S(1)}, f32[2,128,128]{2,1,0:T(8,128)S(1)}, u32[]{:S(2)}, u32[]{:S(2)}) collective-permute-start(f32[2,128,128]{2,1,0:T(8,128)S(1)} %join.2), channel_id=1, source_target_pairs={{0,8},{4,12},{8,0},{12,4},{1,9},{5,13},{9,1},{13,5},{2,10},{6,14},... | collective-permute-start | bytes 393224 | tf_op jit(solution)/shard_map/ppermute | solution.py:252
  17.6 1.6 %local.7.refs_3_ = f32[128,4096]{1,0:T(8,128)S(1)} custom-call(bf16[4096,512]{1,0:T(8,128)(2,1)S(1)} %get-tuple-element.14.refs_0_.refs_1_, bf16[4096,512]{1,0:T(8,128)(2,1)S(1)} %get-tuple-element.15.refs_1_, bf16[4,128,4096]{2,1,0:T(8,128)(2,1)S(1)} %get-tuple-element.16.refs_2_, bf16[4,16,128,128]{3,2,1,0:T(8,128)(2,1)S(1)} %get-tuple-element.12.refs_0_.refs_3_, ...), custom_call_target="tpu_custom_call" | custom-call | tf_op jit(solution)/shard_map/local/pallas_call | solution.py:310
  19.2 1.6 %local.5.refs_3_ = f32[128,4096]{1,0:T(8,128)S(1)} custom-call(bf16[4096,512]{1,0:T(8,128)(2,1)S(1)} %get-tuple-element.14.refs_0_.refs_1_, bf16[4096,512]{1,0:T(8,128)(2,1)S(1)} %get-tuple-element.15.refs_1_, bf16[4,128,4096]{2,1,0:T(8,128)(2,1)S(1)} %get-tuple-element.16.refs_2_, bf16[4,16,128,128]{3,2,1,0:T(8,128)(2,1)S(1)} %get-tuple-element.12.refs_0_.refs_3_, ...), custom_call_target="tpu_custom_call" | custom-call | tf_op jit(solution)/shard_map/local/pallas_call | solution.py:310
  20.8 1.6 %local.4.refs_2_ = f32[128,4096]{1,0:T(8,128)S(1)} custom-call(bf16[4096,512]{1,0:T(8,128)(2,1)S(1)} %get-tuple-element.14.refs_0_.refs_1_, bf16[4096,512]{1,0:T(8,128)(2,1)S(1)} %get-tuple-element.15.refs_1_, bf16[4,128,4096]{2,1,0:T(8,128)(2,1)S(1)} %get-tuple-element.16.refs_2_, bf16[4,16,128,128]{3,2,1,0:T(8,128)(2,1)S(1)} %get-tuple-element.12.refs_0_.refs_3_, ...), custom_call_target="tpu_custom_call" | custom-call | tf_op jit(solution)/shard_map/local/pallas_call | solution.py:310
  22.5 0.0 collective-permute-done.3.refs_4_
  22.5 1.7 %remote.2.refs_5_ = bf16[4096,512]{1,0:T(8,128)(2,1)} custom-call(f32[128,4096]{1,0:T(8,128)S(1)} %get-tuple-element.13.refs_4_.after_ref.refs_0_, bf16[4096,512]{1,0:T(8,128)(2,1)S(1)} %get-tuple-element.14.refs_0_.refs_1_, f32[128,4096]{1,0:T(8,128)S(1)} %local.6.after_ref.refs_2_, f32[128,4096]{1,0:T(8,128)S(1)} %local.7.refs_3_, ...), custom_call_target="tpu_custom_call" | custom-call | tf_op jit(solution)/shard_map/remote/pallas_call | solution.py:325
  24.2 1.2 %collective-permute-done.2.refs_4_ = f32[2,128,128]{2,1,0:T(8,128)S(1)} collective-permute-done((f32[2,128,128]{2,1,0:T(8,128)S(1)}, f32[2,128,128]{2,1,0:T(8,128)S(1)}, u32[]{:S(2)}, u32[]{:S(2)}) %collective-permute-start.2) | collective-permute-done | bytes 131104 | tf_op jit(solution)/shard_map/ppermute | solution.py:252
  25.3 1.7 %remote.3 = bf16[4096,512]{1,0:T(8,128)(2,1)} custom-call(f32[128,4096]{1,0:T(8,128)S(1)} %get-tuple-element.13.refs_4_.after_ref.refs_0_, bf16[4096,512]{1,0:T(8,128)(2,1)S(1)} %get-tuple-element.14.refs_0_.refs_1_, f32[128,4096]{1,0:T(8,128)S(1)} %local.4.refs_2_, f32[128,4096]{1,0:T(8,128)S(1)} %local.5.refs_3_, ...), custom_call_target="tpu_custom_call", output_to_operand_aliasing={{}: (5, {})} | custom-call | tf_op jit(solution)/shard_map/remote/pallas_call | solution.py:325
  (2 shorter events, 0.0 us)
Async XLA Ops:
  4.2 7.5 %collective-permute-start.1 = (f32[2,128,128]{2,1,0:T(8,128)S(1)}, f32[2,128,128]{2,1,0:T(8,128)S(1)}, u32[]{:S(2)}, u32[]{:S(2)}) collective-permute-start(f32[2,128,128]{2,1,0:T(8,128)S(1)} %get-tuple-element.18.left_ref), channel_id=1, source_target_pairs={{0,4},{4,0},{8,12},{12,8},{1,5},{5,1},{9,13},{13,9},{2,6},{6,2},{1... | collective-permute-start | bytes 393224 | tf_op jit(solution)/shard_map/ppermute | solution.py:252
  7.3 9.1 %collective-permute-start = (f32[2,128,128]{2,1,0:T(8,128)S(1)}, f32[2,128,128]{2,1,0:T(8,128)S(1)}, u32[]{:S(2)}, u32[]{:S(2)}) collective-permute-start(f32[2,128,128]{2,1,0:T(8,128)S(1)} %get-tuple-element.17.left_ref), channel_id=1, source_target_pairs={{0,4},{4,0},{8,12},{12,8},{1,5},{5,1},{9,13},{13,9},{2,6},{6,2},{1... | collective-permute-start | bytes 393224 | tf_op jit(solution)/shard_map/ppermute | solution.py:252
  11.7 10.8 %collective-permute-start.3 = (f32[2,128,128]{2,1,0:T(8,128)S(1)}, f32[2,128,128]{2,1,0:T(8,128)S(1)}, u32[]{:S(2)}, u32[]{:S(2)}) collective-permute-start(f32[2,128,128]{2,1,0:T(8,128)S(1)} %join.3), channel_id=1, source_target_pairs={{0,8},{4,12},{8,0},{12,4},{1,9},{5,13},{9,1},{13,5},{2,10},{6,14},... | collective-permute-start | bytes 393224 | tf_op jit(solution)/shard_map/ppermute | solution.py:252
  16.4 8.9 %collective-permute-start.2 = (f32[2,128,128]{2,1,0:T(8,128)S(1)}, f32[2,128,128]{2,1,0:T(8,128)S(1)}, u32[]{:S(2)}, u32[]{:S(2)}) collective-permute-start(f32[2,128,128]{2,1,0:T(8,128)S(1)} %join.2), channel_id=1, source_target_pairs={{0,8},{4,12},{8,0},{12,4},{1,9},{5,13},{9,1},{13,5},{2,10},{6,14},... | collective-permute-start | bytes 393224 | tf_op jit(solution)/shard_map/ppermute | solution.py:252

commit v7 on v6

--- a/solution.py
+++ b/solution.py
@@ -123,10 +123,10 @@
     large.wait()
 
 
-def local_kernel(head, place, local_bits, *refs):
+def local_kernel(head, place, local_bits, last_level, *refs):
     query_ref, key_ref, turned_ref, left_ref, weight_ref = refs[:5]
-    state_refs = refs[5:-2]
-    part_ref, tile_ref = refs[-2:]
+    state_refs = refs[5:-3]
+    part_ref, ahead_ref, tile_ref = refs[-3:]
     token_count = query_ref.shape[0]
     block_count = token_count // BLOCK
     columns = slice(head * LANES, (head + 1) * LANES)
@@ -160,6 +160,9 @@
             weights = jnp.where(lane_tile == tile, chosen, tile_ref[slot, tile : tile + 1, :])
             rows.append(scores[tile * ROWS : (tile + 1) * ROWS] * weights)
         return jnp.concatenate(rows, axis=0).astype(jnp.bfloat16)
+
+    def scaled(query, level, start):
+        return (query.astype(jnp.float32) * level_row(level, start, BLOCK)).astype(jnp.bfloat16)
 
     def begin(block):
         rows = slice(block * BLOCK, (block + 1) * BLOCK)
@@ -184,9 +187,9 @@
             if block >> bit & 1
         ]
         for level, sibling in terms + states:
-            scaled = query.astype(jnp.float32) * level_row(level, start, BLOCK)
-            right.append(scaled.astype(jnp.bfloat16))
+            right.append(scaled(query, level, start))
             left.append(sibling)
+        ahead_ref[:, rows] = scaled(query, last_level, start)
         part_ref[:, rows] = jnp.dot(
             jnp.concatenate(left, axis=1), jnp.concatenate(right, axis=0),
             preferred_element_type=jnp.float32,
@@ -195,30 +198,27 @@
     pipelined(list(range(block_count)), begin, finish, DEPTH)
 
 
-def remote_kernel(heads, level, *refs):
+def remote_kernel(heads, *refs):
     count = len(heads)
-    weight_ref, query_ref = refs[:2]
-    part_refs = refs[2 : 2 + count]
-    state_ref = refs[2 + count]
+    part_refs = refs[:count]
+    ahead_refs = refs[count : 2 * count]
+    state_ref = refs[2 * count]
     out_hbm, buffer, sems = refs[-3:]
-    token_count = weight_ref.shape[1]
+    token_count = buffer.shape[0]
     size = token_count // PIECES
     states = [state_ref[place].astype(jnp.bfloat16) for place in range(count)]
     copies = []
 
     def begin(unit):
         start, place = unit
-        columns = slice(heads[place] * LANES, (heads[place] + 1) * LANES)
-        return lax.dot_general(
-            states[place], query_ref[start : start + BLOCK, columns], ROW_BY_ROW,
-            preferred_element_type=jnp.float32,
+        return jnp.dot(
+            states[place], ahead_refs[place][:, start : start + BLOCK], preferred_element_type=jnp.float32
         )
 
     def finish(unit, product):
         start, place = unit
         rows = slice(start, start + BLOCK)
-        row = heads[place] * SLOT + level
-        result = part_refs[place][:, rows] + product * weight_ref[row : row + 1, rows]
+        result = part_refs[place][:, rows] + product
         buffer[rows, place * LANES : (place + 1) * LANES] = jnp.transpose(result.astype(buffer.dtype))
         if place + 1 == count and (start + BLOCK) % size == 0:
             piece = pl.ds(start + BLOCK - size, size)
@@ -300,30 +300,33 @@
     )(lefts, queries, in_hbm(token_rows[None, :]), in_hbm(jnp.transpose(weight_table, (2, 1, 0))))
 
     received = [[exchange(total, 0)] for total in totals]
-    parts = []
-    after = weights
+    parts, aheads = [], []
     for index, total in enumerate(totals):
         for bit in range(1, bit_count):
-            total = join(total, received[index][-1], after)
+            total = join(total, received[index][-1], weights)
             received[index].append(exchange(total, bit))
         for head in range(index * group, (index + 1) * group):
-            parts += pl.pallas_call(
-                lambda *refs, head=head: local_kernel(head, head % group, local_bits, *refs),
+            results = pl.pallas_call(
+                lambda *refs, head=head: local_kernel(head, head % group, local_bits, local_bits + bit_count, *refs),
                 in_specs=[VMEM] * (5 + bit_count - 1),
-                out_specs=[VMEM],
-                out_shape=[shape((width, token_count), jnp.float32)],
+                out_specs=[VMEM] * 2,
+                out_shape=[
+                    shape((width, token_count), jnp.float32),
+                    shape((width, token_count), jnp.bfloat16),
+                ],
                 scratch_shapes=[pltpu.VMEM((2 * block_count, TILES, HALF), jnp.float32)],
                 compiler_params=params,
                 name="local",
             )(query, keys, turned, lefts, weights, *received[index][:-1])
-        after = parts[0]
+            parts.append(results[0])
+            aheads.append(results[1])
 
     out = None
     for index, arrived in enumerate(received):
         heads = tuple(range(index * group, (index + 1) * group))
-        operands = [weights, query] + [parts[head] for head in heads] + [arrived[-1]]
+        operands = [parts[head] for head in heads] + [aheads[head] for head in heads] + [arrived[-1]]
         out = pl.pallas_call(
-            lambda *refs, heads=heads: remote_kernel(heads, local_bits + bit_count, *refs),
+            lambda *refs, heads=heads: remote_kernel(heads, *refs),
             in_specs=[VMEM] * len(operands) + ([] if out is None else [HBM]),
             out_specs=HBM,
             out_shape=whole,

time: 27.3 us -> 27.8 us (1.018)
  starting transfers between devices: 7.45 us -> 9.08 us
  waiting for transfers between devices: 3.18 us -> 2.01 us
    ppermute x4, starting transfers between devices: 7.45 us -> 9.08 us  [exchange(): lax.ppermute(total, 'ctx', [(device, device ^ 2 ** bit) for device in ran...]
    ppermute x4, waiting for transfers between devices: 3.18 us -> 2.01 us  [exchange(): lax.ppermute(total, 'ctx', [(device, device ^ 2 ** bit) for device in ran...]
  transfers between devices with their start and end apart: 4 -> 4, of which waited for: 2 -> 1; matrix products, arithmetic and copies ran while one was open for 0% -> 0% of each run, Pallas kernels for 39% -> 38%
where the time goes in v7:
time: 27.8 us; the launch traced here: 27.6 us
  Pallas kernels  16.4 us (59%)
  starting transfers between devices  9.08 us (33%)
  waiting for transfers between devices  2.01 us (7%)
    ppermute x4, starting transfers between devices, exchange(): lax.ppermute(total, 'ctx', [(device, device ^ 2 ** bit) for device in ran...  9.08 us
    pallas_call x4, Pallas kernels, body(): pl.pallas_call(lambda *refs, head=head: local_kernel(head, head % group,...  6.58 us
    pallas_call x1, Pallas kernels, body(): pl.pallas_call(totals_kernel, in_specs=[HBM] * 2, out_specs=[VMEM] * (3 +...  4.19 us
    pallas_call x2, Pallas kernels, body(): pl.pallas_call(lambda *refs, heads=heads: remote_kernel(heads, *refs), in...  3.36 us
    pallas_call x1, Pallas kernels, body(): pl.pallas_call(lambda *refs: prepare_kernel(local_bits, *refs), in_specs=...  2.26 us
    ppermute x4, waiting for transfers between devices, exchange(): lax.ppermute(total, 'ctx', [(device, device ^ 2 ** bit) for device in ran...  2.01 us
  transfers between devices with their start and end apart: 4, of which 1 were waited for; matrix products, arithmetic and copies ran while one was open for 0% of the time, Pallas kernels for 38%

profile of v7, /device:TPU:0, one launch (start us, length us, event | category | flops | bytes accessed | tf_op | source)
XLA Modules:
  0.0 27.6 jit_solution(13475096143650975645)
XLA Ops:
  0.0 4.2 %totals.1 = (bf16[4096,512]{1,0:T(8,128)(2,1)S(1)}, bf16[4,128,4096]{2,1,0:T(8,128)(2,1)S(1)}, bf16[4,16,128,128]{3,2,1,0:T(8,128)(2,1)S(1)}, f32[2,128,128]{2,1,0:T(8,128)S(1)}, f32[2,128,128]{2,1,0:T(8,128)S(1)}) custom-call(bf16[4096,512]{1,0:T(8,128)(2,1)} %key_hbm.1, bf16[4096,512]{1,0:T(8,128)(2,1)} %value_hbm.1), custom_call_target="tpu_custom_call" | custom-call | tf_op jit(solution)/shard_map/totals/pallas_call | solution.py:270
  4.2 3.1 %collective-permute-start.2 = (f32[2,128,128]{2,1,0:T(8,128)S(1)}, f32[2,128,128]{2,1,0:T(8,128)S(1)}, u32[]{:S(2)}, u32[]{:S(2)}) collective-permute-start(f32[2,128,128]{2,1,0:T(8,128)S(1)} %get-tuple-element.30.left_ref), channel_id=1, source_target_pairs={{0,4},{4,0},{8,12},{12,8},{1,5},{5,1},{9,13},{13,9},{2,6},{6,2},{1... | collective-permute-start | bytes 393224 | tf_op jit(solution)/shard_map/ppermute | solution.py:252
  7.3 0.1 collective-permute-start
  7.4 2.3 %prepare.1 = (f32[128,4096]{1,0:T(8,128)S(1)}, bf16[4096,512]{1,0:T(8,128)(2,1)S(1)}) custom-call(bf16[4,16,128,128]{3,2,1,0:T(8,128)(2,1)S(1)} %get-tuple-element.20.refs_0_.refs_3_, bf16[4096,512]{1,0:T(8,128)(2,1)} %refs_1_.1, s32[1,4096]{1,0:T(1,128)} %bitcast.3, f32[21,4,64]{2,1,0:T(4,128)} %bitcast.2), custom_call_target="tpu_custom_call" | custom-call | tf_op jit(solution)/shard_map/prepare/pallas_call | solution.py:288
  9.7 2.0 %collective-permute-done.2.refs_5_.right_ref = f32[2,128,128]{2,1,0:T(8,128)S(1)} collective-permute-done((f32[2,128,128]{2,1,0:T(8,128)S(1)}, f32[2,128,128]{2,1,0:T(8,128)S(1)}, u32[]{:S(2)}, u32[]{:S(2)}) %collective-permute-start.2) | collective-permute-done | bytes 131104 | tf_op jit(solution)/shard_map/ppermute | solution.py:252
  11.7 3.1 %collective-permute-start.3 = (f32[2,128,128]{2,1,0:T(8,128)S(1)}, f32[2,128,128]{2,1,0:T(8,128)S(1)}, u32[]{:S(2)}, u32[]{:S(2)}) collective-permute-start(f32[2,128,128]{2,1,0:T(8,128)S(1)} %join.3), channel_id=1, source_target_pairs={{0,8},{4,12},{8,0},{12,4},{1,9},{5,13},{9,1},{13,5},{2,10},{6,14},... | collective-permute-start | bytes 393224 | tf_op jit(solution)/shard_map/ppermute | solution.py:252
  14.8 0.0 collective-permute-done.refs_5_.right_ref
  14.8 2.8 %collective-permute-start.1 = (f32[2,128,128]{2,1,0:T(8,128)S(1)}, f32[2,128,128]{2,1,0:T(8,128)S(1)}, u32[]{:S(2)}, u32[]{:S(2)}) collective-permute-start(f32[2,128,128]{2,1,0:T(8,128)S(1)} %join.2), channel_id=1, source_target_pairs={{0,8},{4,12},{8,0},{12,4},{1,9},{5,13},{9,1},{13,5},{2,10},{6,14},... | collective-permute-start | bytes 393224 | tf_op jit(solution)/shard_map/ppermute | solution.py:252
  17.6 1.6 %local.7 = (f32[128,4096]{1,0:T(8,128)S(1)}, bf16[128,4096]{1,0:T(8,128)(2,1)S(1)}) custom-call(bf16[4096,512]{1,0:T(8,128)(2,1)S(1)} %get-tuple-element.21.refs_0_, bf16[4096,512]{1,0:T(8,128)(2,1)S(1)} %get-tuple-element.22.refs_1_, bf16[4,128,4096]{2,1,0:T(8,128)(2,1)S(1)} %get-tuple-element.23.refs_2_, ...), custom_call_target="tpu_custom_call" | custom-call | tf_op jit(solution)/shard_map/local/pallas_call | solution.py:309
  19.2 1.6 %local.6 = (f32[128,4096]{1,0:T(8,128)S(1)}, bf16[128,4096]{1,0:T(8,128)(2,1)S(1)}) custom-call(bf16[4096,512]{1,0:T(8,128)(2,1)S(1)} %get-tuple-element.21.refs_0_, bf16[4096,512]{1,0:T(8,128)(2,1)S(1)} %get-tuple-element.22.refs_1_, bf16[4,128,4096]{2,1,0:T(8,128)(2,1)S(1)} %get-tuple-element.23.refs_2_, ...), custom_call_target="tpu_custom_call" | custom-call | tf_op jit(solution)/shard_map/local/pallas_call | solution.py:309
  20.9 1.6 %local.5 = (f32[128,4096]{1,0:T(8,128)S(1)}, bf16[128,4096]{1,0:T(8,128)(2,1)S(1)}) custom-call(bf16[4096,512]{1,0:T(8,128)(2,1)S(1)} %get-tuple-element.21.refs_0_, bf16[4096,512]{1,0:T(8,128)(2,1)S(1)} %get-tuple-element.22.refs_1_, bf16[4,128,4096]{2,1,0:T(8,128)(2,1)S(1)} %get-tuple-element.23.refs_2_, ...), custom_call_target="tpu_custom_call" | custom-call | tf_op jit(solution)/shard_map/local/pallas_call | solution.py:309
  22.6 1.6 %local.4 = (f32[128,4096]{1,0:T(8,128)S(1)}, bf16[128,4096]{1,0:T(8,128)(2,1)S(1)}) custom-call(bf16[4096,512]{1,0:T(8,128)(2,1)S(1)} %get-tuple-element.21.refs_0_, bf16[4096,512]{1,0:T(8,128)(2,1)S(1)} %get-tuple-element.22.refs_1_, bf16[4,128,4096]{2,1,0:T(8,128)(2,1)S(1)} %get-tuple-element.23.refs_2_, ...), custom_call_target="tpu_custom_call" | custom-call | tf_op jit(solution)/shard_map/local/pallas_call | solution.py:309
  24.2 0.0 collective-permute-done.3.refs_4_
  24.2 1.7 %remote.2.refs_5_ = bf16[4096,512]{1,0:T(8,128)(2,1)} custom-call(f32[128,4096]{1,0:T(8,128)S(1)} %get-tuple-element.31.refs_0_, f32[128,4096]{1,0:T(8,128)S(1)} %get-tuple-element.32.refs_1_, bf16[128,4096]{1,0:T(8,128)(2,1)S(1)} %get-tuple-element.33.refs_2_, bf16[128,4096]{1,0:T(8,128)(2,1)S(1)} %get-tuple-element.34.refs_3_, ...), custom_call_target="tpu_custom_call" | custom-call | tf_op jit(solution)/shard_map/remote/pallas_call | solution.py:328
  25.9 0.0 collective-permute-done.1.refs_4_
  25.9 1.7 %remote.3 = bf16[4096,512]{1,0:T(8,128)(2,1)} custom-call(f32[128,4096]{1,0:T(8,128)S(1)} %get-tuple-element.26.refs_0_, f32[128,4096]{1,0:T(8,128)S(1)} %get-tuple-element.27.refs_1_, bf16[128,4096]{1,0:T(8,128)(2,1)S(1)} %get-tuple-element.28.refs_2_, bf16[128,4096]{1,0:T(8,128)(2,1)S(1)} %get-tuple-element.29.refs_3_, ...), custom_call_target="tpu_custom_call", output_to_operand_aliasing={{}: (5, {})} | custom-call | tf_op jit(solution)/shard_map/remote/pallas_call | solution.py:328
  (2 shorter events, 0.0 us)
Async XLA Ops:
  4.2 7.5 %collective-permute-start.2 = (f32[2,128,128]{2,1,0:T(8,128)S(1)}, f32[2,128,128]{2,1,0:T(8,128)S(1)}, u32[]{:S(2)}, u32[]{:S(2)}) collective-permute-start(f32[2,128,128]{2,1,0:T(8,128)S(1)} %get-tuple-element.30.left_ref), channel_id=1, source_target_pairs={{0,4},{4,0},{8,12},{12,8},{1,5},{5,1},{9,13},{13,9},{2,6},{6,2},{1... | collective-permute-start | bytes 393224 | tf_op jit(solution)/shard_map/ppermute | solution.py:252
  7.3 7.5 %collective-permute-start = (f32[2,128,128]{2,1,0:T(8,128)S(1)}, f32[2,128,128]{2,1,0:T(8,128)S(1)}, u32[]{:S(2)}, u32[]{:S(2)}) collective-permute-start(f32[2,128,128]{2,1,0:T(8,128)S(1)} %get-tuple-element.25.left_ref), channel_id=1, source_target_pairs={{0,4},{4,0},{8,12},{12,8},{1,5},{5,1},{9,13},{13,9},{2,6},{6,2},{1... | collective-permute-start | bytes 393224 | tf_op jit(solution)/shard_map/ppermute | solution.py:252
  11.7 12.5 %collective-permute-start.3 = (f32[2,128,128]{2,1,0:T(8,128)S(1)}, f32[2,128,128]{2,1,0:T(8,128)S(1)}, u32[]{:S(2)}, u32[]{:S(2)}) collective-permute-start(f32[2,128,128]{2,1,0:T(8,128)S(1)} %join.3), channel_id=1, source_target_pairs={{0,8},{4,12},{8,0},{12,4},{1,9},{5,13},{9,1},{13,5},{2,10},{6,14},... | collective-permute-start | bytes 393224 | tf_op jit(solution)/shard_map/ppermute | solution.py:252
  14.8 11.1 %collective-permute-start.1 = (f32[2,128,128]{2,1,0:T(8,128)S(1)}, f32[2,128,128]{2,1,0:T(8,128)S(1)}, u32[]{:S(2)}, u32[]{:S(2)}) collective-permute-start(f32[2,128,128]{2,1,0:T(8,128)S(1)} %join.2), channel_id=1, source_target_pairs={{0,8},{4,12},{8,0},{12,4},{1,9},{5,13},{9,1},{13,5},{2,10},{6,14},... | collective-permute-start | bytes 393224 | tf_op jit(solution)/shard_map/ppermute | solution.py:252

commit v8 on v6

--- a/solution.py
+++ b/solution.py
@@ -82,7 +82,7 @@
         block, head = unit
         rows = slice(block * BLOCK, (block + 1) * BLOCK)
         turned = jnp.transpose(value_ref[rows, head * LANES : (head + 1) * LANES])
-        turned_ref[head, :, rows] = turned
+        turned_ref[head, block] = turned
         return turned
 
     def finish(unit, turned):
@@ -177,7 +177,7 @@
             jnp.concatenate([low, across], axis=1),
             jnp.concatenate([jnp.zeros_like(low), high], axis=1),
         ]
-        left = [turned_ref[head, :, rows]]
+        left = [turned_ref[head, block]]
         terms = [
             (BLOCK_BITS + 1 + bit, left_ref[head, (block >> bit << bit) - 1])
             for bit in range(block_count.bit_length() - 1)
@@ -187,7 +187,7 @@
             scaled = query.astype(jnp.float32) * level_row(level, start, BLOCK)
             right.append(scaled.astype(jnp.bfloat16))
             left.append(sibling)
-        part_ref[:, rows] = jnp.dot(
+        part_ref[block] = jnp.dot(
             jnp.concatenate(left, axis=1), jnp.concatenate(right, axis=0),
             preferred_element_type=jnp.float32,
         )
@@ -218,7 +218,7 @@
         start, place = unit
         rows = slice(start, start + BLOCK)
         row = heads[place] * SLOT + level
-        result = part_refs[place][:, rows] + product * weight_ref[row : row + 1, rows]
+        result = part_refs[place][start // BLOCK] + product * weight_ref[row : row + 1, rows]
         buffer[rows, place * LANES : (place + 1) * LANES] = jnp.transpose(result.astype(buffer.dtype))
         if place + 1 == count and (start + BLOCK) % size == 0:
             piece = pl.ds(start + BLOCK - size, size)
@@ -273,7 +273,7 @@
         out_specs=[VMEM] * (3 + GROUPS),
         out_shape=[
             whole,
-            shape((head_count, width, token_count), jnp.bfloat16),
+            shape((head_count, block_count, width, BLOCK), jnp.bfloat16),
             shape((head_count, block_count, width, width), jnp.bfloat16),
             *[shape((group, width, width), jnp.float32)] * GROUPS,
         ],
@@ -311,7 +311,7 @@
                 lambda *refs, head=head: local_kernel(head, head % group, local_bits, *refs),
                 in_specs=[VMEM] * (5 + bit_count - 1),
                 out_specs=[VMEM],
-                out_shape=[shape((width, token_count), jnp.float32)],
+                out_shape=[shape((block_count, width, BLOCK), jnp.float32)],
                 scratch_shapes=[pltpu.VMEM((2 * block_count, TILES, HALF), jnp.float32)],
                 compiler_params=params,
                 name="local",

time: 27.3 us -> 27.2 us (level)
  transfers between devices with their start and end apart: 4 -> 4, of which waited for: 2 -> 2; matrix products, arithmetic and copies ran while one was open for 0% -> 0% of each run, Pallas kernels for 39% -> 38%
where the time goes in v8:
time: 27.2 us; the launch traced here: 27 us
  Pallas kernels  16.2 us (60%)
  starting transfers between devices  7.46 us (27%)
  waiting for transfers between devices  3.21 us (12%)
    ppermute x4, starting transfers between devices, exchange(): lax.ppermute(total, 'ctx', [(device, device ^ 2 ** bit) for device in ran...  7.46 us
    pallas_call x4, Pallas kernels, body(): pl.pallas_call(lambda *refs, head=head: local_kernel(head, head % group,...  6.42 us
    pallas_call x1, Pallas kernels, body(): pl.pallas_call(totals_kernel, in_specs=[HBM] * 2, out_specs=[VMEM] * (3 +...  4.16 us
    pallas_call x2, Pallas kernels, body(): pl.pallas_call(lambda *refs, heads=heads: remote_kernel(heads, local_bits...  3.37 us
    ppermute x4, waiting for transfers between devices, exchange(): lax.ppermute(total, 'ctx', [(device, device ^ 2 ** bit) for device in ran...  3.21 us
    pallas_call x1, Pallas kernels, body(): pl.pallas_call(lambda *refs: prepare_kernel(local_bits, *refs), in_specs=...  2.26 us
  transfers between devices with their start and end apart: 4, of which 2 were waited for; matrix products, arithmetic and copies ran while one was open for 0% of the time, Pallas kernels for 38%

profile of v8, /device:TPU:0, one launch (start us, length us, event | category | flops | bytes accessed | tf_op | source)
XLA Modules:
  0.0 27.0 jit_solution(8690078025937450772)
XLA Ops:
  0.0 4.2 %totals.1 = (bf16[4096,512]{1,0:T(8,128)(2,1)S(1)}, bf16[4,16,128,256]{3,2,1,0:T(8,128)(2,1)S(1)}, bf16[4,16,128,128]{3,2,1,0:T(8,128)(2,1)S(1)}, f32[2,128,128]{2,1,0:T(8,128)S(1)}, f32[2,128,128]{2,1,0:T(8,128)S(1)}) custom-call(bf16[4096,512]{1,0:T(8,128)(2,1)} %key_hbm.1, bf16[4096,512]{1,0:T(8,128)(2,1)} %value_hbm.1), custom_call_target="tpu_custom_call" | custom-call | tf_op jit(solution)/shard_map/totals/pallas_call | solution.py:270
  4.2 3.1 %collective-permute-start.1 = (f32[2,128,128]{2,1,0:T(8,128)S(1)}, f32[2,128,128]{2,1,0:T(8,128)S(1)}, u32[]{:S(2)}, u32[]{:S(2)}) collective-permute-start(f32[2,128,128]{2,1,0:T(8,128)S(1)} %get-tuple-element.18.left_ref), channel_id=1, source_target_pairs={{0,4},{4,0},{8,12},{12,8},{1,5},{5,1},{9,13},{13,9},{2,6},{6,2},{1... | collective-permute-start | bytes 393224 | tf_op jit(solution)/shard_map/ppermute | solution.py:252
  7.3 0.1 collective-permute-start
  7.4 2.3 %prepare.1 = (f32[128,4096]{1,0:T(8,128)S(1)}, bf16[4096,512]{1,0:T(8,128)(2,1)S(1)}) custom-call(bf16[4,16,128,128]{3,2,1,0:T(8,128)(2,1)S(1)} %get-tuple-element.12.refs_0_.refs_3_, bf16[4096,512]{1,0:T(8,128)(2,1)} %refs_1_.1, s32[1,4096]{1,0:T(1,128)} %bitcast.3, f32[21,4,64]{2,1,0:T(4,128)} %bitcast.2), custom_call_target="tpu_custom_call" | custom-call | tf_op jit(solution)/shard_map/prepare/pallas_call | solution.py:288
  9.6 2.0 %collective-permute-done.1.refs_5_.right_ref = f32[2,128,128]{2,1,0:T(8,128)S(1)} collective-permute-done((f32[2,128,128]{2,1,0:T(8,128)S(1)}, f32[2,128,128]{2,1,0:T(8,128)S(1)}, u32[]{:S(2)}, u32[]{:S(2)}) %collective-permute-start.1) | collective-permute-done | bytes 131104 | tf_op jit(solution)/shard_map/ppermute | solution.py:252
  11.7 3.1 %collective-permute-start.3 = (f32[2,128,128]{2,1,0:T(8,128)S(1)}, f32[2,128,128]{2,1,0:T(8,128)S(1)}, u32[]{:S(2)}, u32[]{:S(2)}) collective-permute-start(f32[2,128,128]{2,1,0:T(8,128)S(1)} %join.3), channel_id=1, source_target_pairs={{0,8},{4,12},{8,0},{12,4},{1,9},{5,13},{9,1},{13,5},{2,10},{6,14},... | collective-permute-start | bytes 393224 | tf_op jit(solution)/shard_map/ppermute | solution.py:252
  14.8 1.6 %local.6.after_ref.refs_2_ = f32[16,128,256]{2,1,0:T(8,128)S(1)} custom-call(bf16[4096,512]{1,0:T(8,128)(2,1)S(1)} %get-tuple-element.14.refs_0_.refs_1_, bf16[4096,512]{1,0:T(8,128)(2,1)S(1)} %get-tuple-element.15.refs_1_, bf16[4,16,128,256]{3,2,1,0:T(8,128)(2,1)S(1)} %get-tuple-element.16.refs_2_, ...), custom_call_target="tpu_custom_call" | custom-call | tf_op jit(solution)/shard_map/local/pallas_call | solution.py:310
  16.4 0.0 collective-permute-done.refs_5_.right_ref
  16.4 1.2 %collective-permute-start.2 = (f32[2,128,128]{2,1,0:T(8,128)S(1)}, f32[2,128,128]{2,1,0:T(8,128)S(1)}, u32[]{:S(2)}, u32[]{:S(2)}) collective-permute-start(f32[2,128,128]{2,1,0:T(8,128)S(1)} %join.2), channel_id=1, source_target_pairs={{0,8},{4,12},{8,0},{12,4},{1,9},{5,13},{9,1},{13,5},{2,10},{6,14},... | collective-permute-start | bytes 393224 | tf_op jit(solution)/shard_map/ppermute | solution.py:252
  17.6 1.6 %local.7.refs_3_ = f32[16,128,256]{2,1,0:T(8,128)S(1)} custom-call(bf16[4096,512]{1,0:T(8,128)(2,1)S(1)} %get-tuple-element.14.refs_0_.refs_1_, bf16[4096,512]{1,0:T(8,128)(2,1)S(1)} %get-tuple-element.15.refs_1_, bf16[4,16,128,256]{3,2,1,0:T(8,128)(2,1)S(1)} %get-tuple-element.16.refs_2_, bf16[4,16,128,128]{3,2,1,0:T(8,128)(2,1)S(1)} %get-tuple-element.12.refs_0_.refs_3_, ...), custom_call_target="tpu_custom_call" | custom-call | tf_op jit(solution)/shard_map/local/pallas_call | solution.py:310
  19.2 1.6 %local.5.refs_3_ = f32[16,128,256]{2,1,0:T(8,128)S(1)} custom-call(bf16[4096,512]{1,0:T(8,128)(2,1)S(1)} %get-tuple-element.14.refs_0_.refs_1_, bf16[4096,512]{1,0:T(8,128)(2,1)S(1)} %get-tuple-element.15.refs_1_, bf16[4,16,128,256]{3,2,1,0:T(8,128)(2,1)S(1)} %get-tuple-element.16.refs_2_, bf16[4,16,128,128]{3,2,1,0:T(8,128)(2,1)S(1)} %get-tuple-element.12.refs_0_.refs_3_, ...), custom_call_target="tpu_custom_call" | custom-call | tf_op jit(solution)/shard_map/local/pallas_call | solution.py:310
  20.8 1.6 %local.4.refs_2_ = f32[16,128,256]{2,1,0:T(8,128)S(1)} custom-call(bf16[4096,512]{1,0:T(8,128)(2,1)S(1)} %get-tuple-element.14.refs_0_.refs_1_, bf16[4096,512]{1,0:T(8,128)(2,1)S(1)} %get-tuple-element.15.refs_1_, bf16[4,16,128,256]{3,2,1,0:T(8,128)(2,1)S(1)} %get-tuple-element.16.refs_2_, bf16[4,16,128,128]{3,2,1,0:T(8,128)(2,1)S(1)} %get-tuple-element.12.refs_0_.refs_3_, ...), custom_call_target="tpu_custom_call" | custom-call | tf_op jit(solution)/shard_map/local/pallas_call | solution.py:310
  22.4 0.0 collective-permute-done.3.refs_4_
  22.4 1.7 %remote.2.refs_5_ = bf16[4096,512]{1,0:T(8,128)(2,1)} custom-call(f32[128,4096]{1,0:T(8,128)S(1)} %get-tuple-element.13.refs_4_.after_ref.refs_0_, bf16[4096,512]{1,0:T(8,128)(2,1)S(1)} %get-tuple-element.14.refs_0_.refs_1_, f32[16,128,256]{2,1,0:T(8,128)S(1)} %local.6.after_ref.refs_2_, f32[16,128,256]{2,1,0:T(8,128)S(1)} %local.7.refs_3_, ...), custom_call_target="tpu_custom_call" | custom-call | tf_op jit(solution)/shard_map/remote/pallas_call | solution.py:325
  24.1 1.2 %collective-permute-done.2.refs_4_ = f32[2,128,128]{2,1,0:T(8,128)S(1)} collective-permute-done((f32[2,128,128]{2,1,0:T(8,128)S(1)}, f32[2,128,128]{2,1,0:T(8,128)S(1)}, u32[]{:S(2)}, u32[]{:S(2)}) %collective-permute-start.2) | collective-permute-done | bytes 131104 | tf_op jit(solution)/shard_map/ppermute | solution.py:252
  25.3 1.7 %remote.3 = bf16[4096,512]{1,0:T(8,128)(2,1)} custom-call(f32[128,4096]{1,0:T(8,128)S(1)} %get-tuple-element.13.refs_4_.after_ref.refs_0_, bf16[4096,512]{1,0:T(8,128)(2,1)S(1)} %get-tuple-element.14.refs_0_.refs_1_, f32[16,128,256]{2,1,0:T(8,128)S(1)} %local.4.refs_2_, f32[16,128,256]{2,1,0:T(8,128)S(1)} %local.5.refs_3_, ...), custom_call_target="tpu_custom_call", output_to_operand_aliasing={{}: (5, {})} | custom-call | tf_op jit(solution)/shard_map/remote/pallas_call | solution.py:325
  (2 shorter events, 0.0 us)
Async XLA Ops:
  4.2 7.5 %collective-permute-start.1 = (f32[2,128,128]{2,1,0:T(8,128)S(1)}, f32[2,128,128]{2,1,0:T(8,128)S(1)}, u32[]{:S(2)}, u32[]{:S(2)}) collective-permute-start(f32[2,128,128]{2,1,0:T(8,128)S(1)} %get-tuple-element.18.left_ref), channel_id=1, source_target_pairs={{0,4},{4,0},{8,12},{12,8},{1,5},{5,1},{9,13},{13,9},{2,6},{6,2},{1... | collective-permute-start | bytes 393224 | tf_op jit(solution)/shard_map/ppermute | solution.py:252
  7.3 9.1 %collective-permute-start = (f32[2,128,128]{2,1,0:T(8,128)S(1)}, f32[2,128,128]{2,1,0:T(8,128)S(1)}, u32[]{:S(2)}, u32[]{:S(2)}) collective-permute-start(f32[2,128,128]{2,1,0:T(8,128)S(1)} %get-tuple-element.17.left_ref), channel_id=1, source_target_pairs={{0,4},{4,0},{8,12},{12,8},{1,5},{5,1},{9,13},{13,9},{2,6},{6,2},{1... | collective-permute-start | bytes 393224 | tf_op jit(solution)/shard_map/ppermute | solution.py:252
  11.7 10.7 %collective-permute-start.3 = (f32[2,128,128]{2,1,0:T(8,128)S(1)}, f32[2,128,128]{2,1,0:T(8,128)S(1)}, u32[]{:S(2)}, u32[]{:S(2)}) collective-permute-start(f32[2,128,128]{2,1,0:T(8,128)S(1)} %join.3), channel_id=1, source_target_pairs={{0,8},{4,12},{8,0},{12,4},{1,9},{5,13},{9,1},{13,5},{2,10},{6,14},... | collective-permute-start | bytes 393224 | tf_op jit(solution)/shard_map/ppermute | solution.py:252
  16.4 8.9 %collective-permute-start.2 = (f32[2,128,128]{2,1,0:T(8,128)S(1)}, f32[2,128,128]{2,1,0:T(8,128)S(1)}, u32[]{:S(2)}, u32[]{:S(2)}) collective-permute-start(f32[2,128,128]{2,1,0:T(8,128)S(1)} %join.2), channel_id=1, source_target_pairs={{0,8},{4,12},{8,0},{12,4},{1,9},{5,13},{9,1},{13,5},{2,10},{6,14},... | collective-permute-start | bytes 393224 | tf_op jit(solution)/shard_map/ppermute | solution.py:252
